TPU v7x, 128 devices: a whole 4x4x4 slice. The times are simulated.
128 devices in a mesh: seq: 8 (over x, core), exp: 16 (over y, z).
Axes of the slice: x: 4, y: 4, z: 4, core: 2. Of those that a mesh axis runs over, the one named last changes fastest.
Arguments:
- queries: bfloat16 [16, 512, 4096], P('exp', 'seq'), may hold values from -130 to 130
- new_keys: bfloat16 [16, 512, 512], P('exp', 'seq'), may hold values from -6 to 6
- new_values: bfloat16 [16, 512, 512], P('exp', 'seq'), may hold values from -6 to 6
- cache_keys: bfloat16 [16, 4096, 512], P('exp', 'seq'), may hold values from -7 to 7
- cache_values: bfloat16 [16, 4096, 512], P('exp', 'seq'), may hold values from -6 to 6
- cache_len: int32 [16], P('exp'), may hold values from 1024 to 4096, as said below
- residual_in: bfloat16 [16, 512, 2048], P('exp', 'seq'), may hold values from -6 to 6
- out_weight: bfloat16 [4096, 2048], P('seq'), may hold values from -0.09375 to 0.09375
- norm_gain: float32 [2048], replicated, may hold values from 0.25 to 1.75
- router_weight: bfloat16 [2048, 128], replicated, may hold values from -0.125 to 0.125
- expert_ids: int32 [16, 512, 8], P('exp', 'seq'), may hold values from 0 to 127, all different within a row; in each aligned block of 64 rows (0 to 63, 64 to 127, ..., all dimensions but the last counted through in order) at most 6 rows name the same one
- gate_proj: bfloat16 [128, 2048, 768], P(('seq', 'exp')), may hold values from -0.125 to 0.125
- up_proj: bfloat16 [128, 2048, 768], P(('seq', 'exp')), may hold values from -0.125 to 0.125
- down_proj: bfloat16 [128, 768, 2048], P(('seq', 'exp')), may hold values from -0.21875 to 0.21875
Outputs:
- layer_out: bfloat16 [16, 512, 2048], P('exp', 'seq')
Inputs may be any that keep to these rules, and one draw needn't show every extreme that they name: `expert_ids`: among the rows of one device (aligned blocks of 64 tokens of one document) no expert is chosen more than 6 times; every token chooses 8 different experts. `cache_len`: some document fills its whole cache.
All inputs are finite; a program needn't handle non-finite values.
Results may differ from a plain program's by a relative error of at most 0.0042.
Values may be sent and summed in bfloat16 or wider, within the bound.
A program may use at most 128 MiB of HBM per device.

v0:
```python
import jax
import jax.numpy as jnp
from jax import lax
from jax.sharding import PartitionSpec as P

QH = 32
KVH = 4
HD = 128
TOPK = 8


def spread_heads(kv_rows, nseq):
    count = kv_rows.shape[0]
    slots = max(KVH, nseq)
    repeat = slots // KVH
    per_dev = slots // nseq
    heads = kv_rows.reshape(count, KVH, 1, HD)
    heads = jnp.broadcast_to(heads, (count, KVH, repeat, HD))
    return heads.reshape(count, nseq, per_dev * HD)


def expert_token_rows(piece, gate_proj, up_proj, down_proj):
    width = piece.shape[-1]
    rows = piece.reshape(-1, width)
    gate = jnp.dot(rows, gate_proj[0], preferred_element_type=jnp.float32)
    upv = jnp.dot(rows, up_proj[0], preferred_element_type=jnp.float32)
    act = (jax.nn.silu(gate) * upv).astype(jnp.bfloat16)
    result = jnp.dot(act, down_proj[0], preferred_element_type=jnp.float32).astype(jnp.bfloat16)
    return result.reshape(piece.shape)


def attention_per_head(queries, new_keys, new_values, cache_keys, cache_values, length, nseq):
    tokens = queries.shape[1]
    local_q = QH // nseq
    per_dev = max(KVH, nseq) // nseq
    group = local_q // per_dev
    q_split = queries[0].reshape(tokens, nseq, local_q * HD)
    q_all, k_new, v_new, k_old, v_old = (
        lax.all_to_all(q_split, "seq", split_axis=1, concat_axis=0, tiled=True),
        lax.all_to_all(
            spread_heads(new_keys[0], nseq), "seq", split_axis=1, concat_axis=0, tiled=True
        ),
        lax.all_to_all(
            spread_heads(new_values[0], nseq), "seq", split_axis=1, concat_axis=0, tiled=True
        ),
        lax.all_to_all(
            spread_heads(cache_keys[0], nseq), "seq", split_axis=1, concat_axis=0, tiled=True
        ),
        lax.all_to_all(
            spread_heads(cache_values[0], nseq), "seq", split_axis=1, concat_axis=0, tiled=True
        ),
    )
    qtok = q_all.shape[0]
    ncache = k_old.shape[0]
    total = ncache + qtok
    qheads = q_all.reshape(qtok, per_dev, group, HD)
    keys = jnp.concatenate([k_old, k_new], 0)
    value_entries = jnp.concatenate([v_old, v_new], 0)
    block = min(512, qtok)
    scale = 1.0 / jnp.sqrt(jnp.float32(HD))
    kpos = jnp.arange(total, dtype=jnp.int32)[None, :]

    def attend(start):
        scores = (
            jnp.einsum("bpgd,kpd->pgbk", qheads, keys, preferred_element_type=jnp.float32) * scale
        )
        qpos = start + jnp.arange(block, dtype=jnp.int32)[:, None]
        visible = jnp.where(kpos < ncache, kpos < length, kpos - ncache <= qpos)
        scores = jnp.where(visible[None, None], scores, jnp.float32(-1e30))
        peak = jnp.max(scores, axis=-1, keepdims=True)
        expo = jnp.exp(scores - peak)
        weight_matrices = (expo / jnp.sum(expo, axis=-1, keepdims=True)).astype(jnp.bfloat16)
        outs = jnp.einsum(
            "pgbk,kpd->bpgd", weight_matrices, value_entries, preferred_element_type=jnp.float32
        )
        return outs.astype(jnp.bfloat16).reshape(block, local_q * HD)

    starts = jnp.arange(qtok // block, dtype=jnp.int32) * block
    return lax.map(attend, starts).reshape(qtok, local_q * HD)


def body(
    queries,
    new_keys,
    new_values,
    cache_keys,
    cache_values,
    cache_len,
    residual_in,
    out_weight,
    norm_gain,
    router_weight,
    expert_ids,
    gate_proj,
    up_proj,
    down_proj,
):
    nseq = lax.axis_size("seq")
    tokens = queries.shape[1]
    width = residual_in.shape[2]
    length = cache_len[0]
    attn = attention_per_head(queries, new_keys, new_values, cache_keys, cache_values, length, nseq)
    projected = lax.psum_scatter(
        jnp.dot(attn, out_weight, preferred_element_type=jnp.float32),
        "seq",
        scatter_dimension=0,
        tiled=True,
    )
    mixed = residual_in[0].astype(jnp.float32) + projected
    meansq = jnp.mean(mixed * mixed, axis=-1, keepdims=True)
    normed = (mixed / jnp.sqrt(meansq + 1e-06) * norm_gain).astype(jnp.bfloat16)
    logits = jnp.dot(normed, router_weight, preferred_element_type=jnp.float32)
    nexp = router_weight.shape[1]
    chosen = expert_ids[0]
    onehot = chosen[:, :, None] == jnp.arange(nexp, dtype=jnp.int32)[None, None, :]
    picked = jnp.sum(jnp.where(onehot, logits[:, None, :], jnp.float32(0.0)), axis=2)
    expo = jnp.exp(picked)
    gates = expo / jnp.sum(expo, axis=1, keepdims=True)
    capacity = 3 * tokens * TOPK // (2 * nexp)
    flat = chosen.reshape(-1)
    member = (flat[:, None] == jnp.arange(nexp, dtype=jnp.int32)[None, :]).astype(jnp.int32)
    rank = jnp.sum((jnp.cumsum(member, axis=0) - 1) * member, axis=1)
    slot = flat * capacity + rank
    place = slot[:, None] == jnp.arange(nexp * capacity, dtype=jnp.int32)[None, :]
    route = jnp.any(place.reshape(tokens, TOPK, nexp * capacity), axis=1).astype(jnp.bfloat16)
    packed = jnp.einsum("ts,td->sd", route, normed, preferred_element_type=jnp.float32).astype(
        jnp.bfloat16
    )
    outgoing = packed.reshape(nexp, capacity, width)
    result = expert_token_rows(
        lax.all_to_all(outgoing, ("seq", "exp"), split_axis=0, concat_axis=0, tiled=True),
        gate_proj,
        up_proj,
        down_proj,
    )
    back = lax.all_to_all(result, ("seq", "exp"), split_axis=0, concat_axis=0, tiled=True)
    back = back.reshape(nexp * capacity, width)
    gathered = back[slot].reshape(tokens, TOPK, width)
    moe = jnp.sum(gates[:, :, None] * gathered.astype(jnp.float32), axis=1)
    return (mixed + moe).astype(jnp.bfloat16).reshape(1, tokens, width)


def solution(mesh):
    in_specs = (
        P("exp", "seq", None),
        P("exp", "seq", None),
        P("exp", "seq", None),
        P("exp", "seq", None),
        P("exp", "seq", None),
        P("exp"),
        P("exp", "seq", None),
        P("seq", None),
        P(),
        P(),
        P("exp", "seq", None),
        P(("seq", "exp"), None, None),
        P(("seq", "exp"), None, None),
        P(("seq", "exp"), None, None),
    )
    out_specs = P("exp", "seq", None)
    return jax.shard_map(body, mesh=mesh, in_specs=in_specs, out_specs=out_specs, check_vma=False)
```

profile of v0, /device:TPU:1, one launch (start us, length us, event | category | flops | bytes accessed | tf_op | source)
XLA Modules:
  0.0 371.5 jit_solution(14057827935737912503)
XLA Ops:
  6.5 1.0 broadcast_in_dim.110
  7.6 0.7 broadcast_in_dim.111
  8.2 5.8 %all-to-all-start.3 = ((bf16[64,8,128]{2,0,1:T(8,128)(2,1)}), bf16[64,8,128]{2,0,1:T(8,128)(2,1)S(1)}, u32[]{:S(2)}, u32[]{:S(2)}) async-start(bf16[64,8,128]{2,0,1:T(8,128)(2,1)} %bitcast.16), calls=%async_computation.3 | async-start | bytes 262144 | tf_op jit(solution)/shard_map/all_to_all | solution.py:40
  14.0 0.9 broadcast_in_dim.103
  14.9 4.4 %all-to-all-done.3 = bf16[64,8,128]{2,0,1:T(8,128)(2,1)S(1)} async-done(((bf16[64,8,128]{2,0,1:T(8,128)(2,1)}), bf16[64,8,128]{2,0,1:T(8,128)(2,1)S(1)}, u32[]{:S(2)}, u32[]{:S(2)}) %all-to-all-start.3) | async-done | bytes 131104 | tf_op jit(solution)/shard_map/all_to_all | solution.py:40
  19.3 0.7 broadcast_in_dim.104
  19.9 4.1 %all-to-all-start.1 = ((bf16[64,8,128]{2,0,1:T(8,128)(2,1)}), bf16[64,8,128]{2,0,1:T(8,128)(2,1)S(1)}, u32[]{:S(2)}, u32[]{:S(2)}) async-start(bf16[64,8,128]{2,0,1:T(8,128)(2,1)} %bitcast.5), calls=%async_computation.1 | async-start | bytes 262144 | tf_op jit(solution)/shard_map/all_to_all | solution.py:43
  24.1 1.2 copy.69
  25.3 0.9 copy.57
  26.2 3.1 all-to-all-done.1
  29.4 4.9 %all-to-all-start.4 = ((bf16[64,8,512]{2,0,1:T(8,128)(2,1)}), bf16[64,8,512]{2,0,1:T(8,128)(2,1)}, u32[]{:S(2)}, u32[]{:S(2)}) async-start(bf16[64,8,512]{2,0,1:T(8,128)(2,1)} %copy.57), calls=%async_computation.4 | async-start | bytes 1048576 | tf_op jit(solution)/shard_map/all_to_all | solution.py:39
  34.2 2.1 copy.67
  36.3 7.4 %all-to-all-done.4 = bf16[64,8,512]{2,0,1:T(8,128)(2,1)} async-done(((bf16[64,8,512]{2,0,1:T(8,128)(2,1)}), bf16[64,8,512]{2,0,1:T(8,128)(2,1)}, u32[]{:S(2)}, u32[]{:S(2)}) %all-to-all-start.4) | async-done | bytes 524320 | tf_op jit(solution)/shard_map/all_to_all | solution.py:39
  43.7 2.2 broadcast_in_dim.102
  45.9 5.1 %all-to-all-start = ((bf16[512,8,128]{0,2,1:T(8,128)(2,1)}), bf16[512,8,128]{0,2,1:T(8,128)(2,1)}, u32[]{:S(2)}, u32[]{:S(2)}) async-start(bf16[512,8,128]{0,2,1:T(8,128)(2,1)} %bitcast.120), calls=%async_computation | async-start | bytes 2097152 | tf_op jit(solution)/shard_map/all_to_all | solution.py:49
  51.6 2.0 broadcast_in_dim.108
  53.6 1.9 copy.55
  55.5 10.6 %all-to-all-done = bf16[512,8,128]{0,2,1:T(8,128)(2,1)} async-done(((bf16[512,8,128]{0,2,1:T(8,128)(2,1)}), bf16[512,8,128]{0,2,1:T(8,128)(2,1)}, u32[]{:S(2)}, u32[]{:S(2)}) %all-to-all-start) | async-done | bytes 1048608 | tf_op jit(solution)/shard_map/all_to_all | solution.py:49
  66.1 2.2 broadcast_in_dim.109
  68.3 5.1 %all-to-all-start.2 = ((bf16[512,8,128]{2,0,1:T(8,128)(2,1)}), bf16[512,8,128]{2,0,1:T(8,128)(2,1)}, u32[]{:S(2)}, u32[]{:S(2)}) async-start(bf16[512,8,128]{2,0,1:T(8,128)(2,1)} %bitcast.119), calls=%async_computation.2 | async-start | bytes 2097152 | tf_op jit(solution)/shard_map/all_to_all | solution.py:46
  73.4 5.8 %fusion.4 = pred[512,4608]{0,1:T(8,128)(4,1)} fusion(s32[4608]{0:T(1024)S(1)} %iota_add_fusion, pred[4608]{0:T(1024)(128)(4,1)S(1)} %get-tuple-element.19, pred[4608]{0:T(1024)(128)(4,1)S(1)} %get-tuple-element.20), kind=kLoop, calls=%fused_computation.9 | loop fusion | flops 4718592 | bytes 2386944 | tf_op jit(solution)/shard_map/while/body/eval_jaxpr/jit(_where)/select_n | solution.py:68
  79.2 2.0 reshape.243
  81.2 2.4 copy.68
  83.6 4.9 %all-to-all-done.2 = bf16[512,8,128]{2,0,1:T(8,128)(2,1)} async-done(((bf16[512,8,128]{2,0,1:T(8,128)(2,1)}), bf16[512,8,128]{2,0,1:T(8,128)(2,1)}, u32[]{:S(2)}, u32[]{:S(2)}) %all-to-all-start.2) | async-done | bytes 1048608 | tf_op jit(solution)/shard_map/all_to_all | solution.py:46
  88.5 17.7 %fusion.1 = (f32[4,512]{1,0:T(4,128)S(1)}, f32[4608,512,4]{1,0,2:T(8,128)}) fusion(pred[512,4608]{0,1:T(8,128)(4,1)} %fusion.4, bf16[512,4,128]{2,1,0:T(4,128)(2,1)} %reshape.243, bf16[512,1,128]{2,0,1:T(8,128)(2,1)S(1)} %bitcast.128, bf16[4096,1,128]{2,0,1:T(8,128)(2,1)} %bitcast.15), kind=kOutput, calls=%fused_computation.5 | convolution fusion | flops 2446587904 | bytes 41820160 | tf_op jit(solution)/shard_map/while/body/eval_jaxpr/bpgd,kpd->pgbk/dot_general | solution.py:65
  106.2 16.1 %fusion = f32[4,512]{1,0:T(4,128)S(1)} fusion(f32[4608,512,4]{1,0,2:T(8,128)} %get-tuple-element.18, f32[4,512]{1,0:T(4,128)S(1)} %get-tuple-element.17, pred[512,4608]{0,1:T(8,128)(4,1)S(1)} %copy-done.1), kind=kLoop, calls=%fused_computation.4 | loop fusion | flops 37746688 | bytes 40124416 | tf_op jit(solution)/shard_map/while/body/eval_jaxpr/reduce_sum | solution.py:72
  122.3 18.9 %fusion.14 = bf16[128,4,512]{2,0,1:T(8,128)(2,1)} fusion(f32[4,512]{1,0:T(4,128)S(1)} %fusion, f32[4,512]{1,0:T(4,128)S(1)} %get-tuple-element.17, f32[4608,512,4]{1,0,2:T(8,128)} %get-tuple-element.18, pred[512,4608]{0,1:T(8,128)(4,1)} %fusion.4, bf16[512,1,128]{0,2,1:T(8,128)(2,1)S(1)} %copy.54, bf16[4096,1,128]{0,2,1:T(8,128)(2,1)} %bitcast.123), kind=kOutput, calls=%fused_computation.22 | convolution fusion | flops 2465726464 | bytes 41828352 | tf_op jit(solution)/shard_map/while/body/eval_jaxpr/pgbk,kpd->bpgd/dot_general | solution.py:73
  141.2 5.0 %fusion.35 = f32[512,2048]{1,0:T(8,128)} fusion(bf16[512,512]{0,1:T(8,128)(2,1)} %bitcast.127, bf16[512,2048]{1,0:T(8,128)(2,1)} %param.21), kind=kOutput, calls=%fused_computation.62 | convolution fusion | flops 1073741824 | bytes 6815744 | tf_op jit(solution)/shard_map/dot_general | solution.py:104
  147.4 0.7 copy-done.4
  148.2 1.0 add_add_fusion
  150.1 32.1 %reduce-scatter.2.cloned.1.call-done = f32[64,2048]{1,0:T(8,128)} async-done(((f32[512,2048]{1,0:T(8,128)}), f32[64,2048]{1,0:T(8,128)}) %reduce-scatter.2.cloned.1.call-update) | async-done | bytes 524304 | tf_op jit(solution)/shard_map/reduce_scatter | solution.py:103
  182.2 1.2 multiply_reduce_fusion
  183.4 1.2 multiply_convert_fusion.1
  184.6 0.7 copy-done.3
  185.3 2.7 convolution_convert_fusion.1
  188.0 6.3 %reshape.247 = bf16[128,6,2048]{2,1,0:T(8,128)(2,1)} reshape(bf16[768,2048]{1,0:T(8,128)(2,1)} %convolution_convert_fusion.1) | data formatting | bytes 6291456 | tf_op jit(solution)/shard_map/reshape | solution.py:129
  194.3 62.5 %all_to_all.97 = bf16[128,6,2048]{2,1,0:T(8,128)(2,1)} all-to-all(bf16[128,6,2048]{2,1,0:T(8,128)(2,1)} %reshape.247), channel_id=1, replica_groups=mesh['seq'=8,'exp'=16] {'seq','exp'}, dimensions={0} | all-to-all | bytes 6291456 | tf_op jit(solution)/shard_map/all_to_all | solution.py:131
  256.7 6.3 %reshape.248 = bf16[768,2048]{1,0:T(8,128)(2,1)} reshape(bf16[128,6,2048]{2,1,0:T(8,128)(2,1)} %all_to_all.97) | data formatting | bytes 6291456 | tf_op jit(solution)/shard_map/reshape | solution.py:24
  263.1 6.9 %fusion.7 = f32[768,768]{1,0:T(8,128)} fusion(bf16[768,2048]{1,0:T(8,128)(2,1)} %reshape.248, bf16[1,2048,768]{2,1,0:T(8,128)(2,1)} %param.26), kind=kOutput, calls=%fused_computation.15 | convolution fusion | flops 2415919104 | bytes 8650752 | tf_op jit(solution)/shard_map/dot_general | solution.py:26
  270.0 11.1 %convolution_convert_fusion = bf16[768,2048]{1,0:T(8,128)(2,1)} fusion(bf16[1,768,2048]{2,1,0:T(8,128)(2,1)S(1)} %copy-done, f32[768,768]{1,0:T(8,128)} %fusion.7, bf16[768,2048]{1,0:T(8,128)(2,1)} %reshape.248, bf16[1,2048,768]{2,1,0:T(8,128)(2,1)} %param.25), kind=kOutput, calls=%fused_computation.12 | convolution fusion | flops 4836950016 | bytes 14942208 | tf_op jit(solution)/shard_map/dot_general | solution.py:28
  281.0 6.3 %reshape.249 = bf16[128,6,2048]{2,1,0:T(8,128)(2,1)} reshape(bf16[768,2048]{1,0:T(8,128)(2,1)} %convolution_convert_fusion) | data formatting | bytes 6291456 | tf_op jit(solution)/shard_map/reshape | solution.py:29
  287.3 6.2 %all-to-all-start.6 = ((bf16[128,6,2048]{2,1,0:T(8,128)(2,1)}), bf16[128,6,2048]{2,1,0:T(8,128)(2,1)}, u32[]{:S(2)}, u32[]{:S(2)}) async-start(bf16[128,6,2048]{2,1,0:T(8,128)(2,1)} %reshape.249), calls=%async_computation.7 | async-start | bytes 8388608 | tf_op jit(solution)/shard_map/all_to_all | solution.py:136
  293.8 1.3 fusion.36
  295.5 49.9 %all-to-all-done.6 = bf16[128,6,2048]{2,1,0:T(8,128)(2,1)} async-done(((bf16[128,6,2048]{2,1,0:T(8,128)(2,1)}), bf16[128,6,2048]{2,1,0:T(8,128)(2,1)}, u32[]{:S(2)}, u32[]{:S(2)}) %all-to-all-start.6) | async-done | bytes 3145760 | tf_op jit(solution)/shard_map/all_to_all | solution.py:136
  345.4 6.3 %reshape.250 = bf16[768,2048]{1,0:T(8,128)(2,1)} reshape(bf16[128,6,2048]{2,1,0:T(8,128)(2,1)} %all-to-all-done.6) | data formatting | bytes 6291456 | tf_op jit(solution)/shard_map/reshape | solution.py:137
  351.8 7.6 %gather_fusion = bf16[512,2048]{1,0:T(8,128)(2,1)} fusion(bf16[768,2048]{1,0:T(8,128)(2,1)} %reshape.250, s32[1024]{0:T(1024)S(1)} %pad_clamp_fusion), kind=kCustom, calls=%fused_computation | custom fusion | bytes 4196352 | tf_op jit(solution)/shard_map/gather | solution.py:138
  359.4 3.4 fusion.5
  362.8 1.8 fusion.25
  (41 shorter events, 3.0 us)
Async XLA Ops:
  6.5 263.4 %copy-start = (bf16[1,768,2048]{2,1,0:T(8,128)(2,1)S(1)}, bf16[1,768,2048]{2,1,0:T(8,128)(2,1)}, u32[]{:S(2)}) copy-start(bf16[1,768,2048]{2,1,0:T(8,128)(2,1)} %param.27) | copy-start | bytes 9437188
  8.2 11.0 %all-to-all-start.3 = ((bf16[64,8,128]{2,0,1:T(8,128)(2,1)}), bf16[64,8,128]{2,0,1:T(8,128)(2,1)S(1)}, u32[]{:S(2)}, u32[]{:S(2)}) async-start(bf16[64,8,128]{2,0,1:T(8,128)(2,1)} %bitcast.16), calls=%async_computation.3 | async-start | bytes 262144 | tf_op jit(solution)/shard_map/all_to_all | solution.py:40
  19.9 9.4 %all-to-all-start.1 = ((bf16[64,8,128]{2,0,1:T(8,128)(2,1)}), bf16[64,8,128]{2,0,1:T(8,128)(2,1)S(1)}, u32[]{:S(2)}, u32[]{:S(2)}) async-start(bf16[64,8,128]{2,0,1:T(8,128)(2,1)} %bitcast.5), calls=%async_computation.1 | async-start | bytes 262144 | tf_op jit(solution)/shard_map/all_to_all | solution.py:43
  29.4 14.4 %all-to-all-start.4 = ((bf16[64,8,512]{2,0,1:T(8,128)(2,1)}), bf16[64,8,512]{2,0,1:T(8,128)(2,1)}, u32[]{:S(2)}, u32[]{:S(2)}) async-start(bf16[64,8,512]{2,0,1:T(8,128)(2,1)} %copy.57), calls=%async_computation.4 | async-start | bytes 1048576 | tf_op jit(solution)/shard_map/all_to_all | solution.py:39
  45.9 20.2 %all-to-all-start = ((bf16[512,8,128]{0,2,1:T(8,128)(2,1)}), bf16[512,8,128]{0,2,1:T(8,128)(2,1)}, u32[]{:S(2)}, u32[]{:S(2)}) async-start(bf16[512,8,128]{0,2,1:T(8,128)(2,1)} %bitcast.120), calls=%async_computation | async-start | bytes 2097152 | tf_op jit(solution)/shard_map/all_to_all | solution.py:49
  68.3 20.2 %all-to-all-start.2 = ((bf16[512,8,128]{2,0,1:T(8,128)(2,1)}), bf16[512,8,128]{2,0,1:T(8,128)(2,1)}, u32[]{:S(2)}, u32[]{:S(2)}) async-start(bf16[512,8,128]{2,0,1:T(8,128)(2,1)} %bitcast.119), calls=%async_computation.2 | async-start | bytes 2097152 | tf_op jit(solution)/shard_map/all_to_all | solution.py:46
  73.4 108.8 %reduce-scatter.2.cloned.1.call-start = ((), (), s32[]{:S(2)}) async-start(), calls=%async_computation.8 | async-start | bytes 4718592 | tf_op jit(solution)/shard_map/reduce_scatter | solution.py:103
  88.5 17.7 %copy-start.1 = (pred[512,4608]{0,1:T(8,128)(4,1)S(1)}, pred[512,4608]{0,1:T(8,128)(4,1)}, u32[]{:S(2)}) copy-start(pred[512,4608]{0,1:T(8,128)(4,1)} %fusion.4) | copy-start | bytes 7077892
  146.1 0.7 copy-start.5
  146.1 36.1 %copy-start.2 = (bf16[1,64,2048]{2,1,0:T(8,128)(2,1)S(1)}, bf16[1,64,2048]{2,1,0:T(8,128)(2,1)}, u32[]{:S(2)}) copy-start(bf16[1,64,2048]{2,1,0:T(8,128)(2,1)} %param.20) | copy-start | bytes 786436
  146.1 37.3 %copy-start.6 = (f32[2048]{0:T(1024)S(1)}, f32[2048]{0:T(1024)}, u32[]{:S(2)}) copy-start(f32[2048]{0:T(1024)} %param.22) | copy-start | bytes 24580
  147.4 0.7 copy-start.4
  184.6 0.7 copy-start.3
  287.3 58.1 %all-to-all-start.6 = ((bf16[128,6,2048]{2,1,0:T(8,128)(2,1)}), bf16[128,6,2048]{2,1,0:T(8,128)(2,1)}, u32[]{:S(2)}, u32[]{:S(2)}) async-start(bf16[128,6,2048]{2,1,0:T(8,128)(2,1)} %reshape.249), calls=%async_computation.7 | async-start | bytes 8388608 | tf_op jit(solution)/shard_map/all_to_all | solution.py:136
Sparse Core Ops, SparseCore 0:
  146.3 35.8 reduce-scatter.1
where the time goes:
time: 374 us; the launch traced here: 371 us
  waiting for transfers between devices  112 us (30%)
  matrix products  63.6 us (17%)
  blocking collectives  62.5 us (17%)
  local copies, waits for them, and re-layouts  55.6 us (15%)
  other arithmetic  32 us (9%)
  starting transfers between devices  31.2 us (8%)
  between operations  14.2 us (4%)
    all_to_all x1, blocking collectives, body(): lax.all_to_all(outgoing, ('seq', 'exp'), split_axis=0, concat_axis=0, til...  62.5 us
    all_to_all x1, waiting for transfers between devices, body(): lax.all_to_all(result, ('seq', 'exp'), split_axis=0, concat_axis=0, tiled...  49.9 us
    reduce_scatter x1, waiting for transfers between devices, body(): lax.psum_scatter(jnp.dot(attn, out_weight, preferred_element_type=jnp.flo...  32.1 us
    dot_general x1, matrix products, attend(): jnp.einsum('pgbk,kpd->bpgd', weight_matrices, value_entries, preferred_el...  18.9 us
    dot_general x1, matrix products, attend(): jnp.einsum('bpgd,kpd->pgbk', qheads, keys, preferred_element_type=jnp.flo...  17.7 us
    reduce_sum x1, other arithmetic, attend(): jnp.sum(expo, axis=-1, keepdims=True)  16.1 us
    broadcast_in_dim x11, local copies, waits for them, and re-layouts, spread_heads(): heads = jnp.broadcast_to(heads, (count, KVH, repeat, HD))  13.6 us
    dot_general x1, matrix products, expert_token_rows(): jnp.dot(act, down_proj[0], preferred_element_type=jnp.float32)  11.1 us
  transfers between devices with their start and end apart: 7, of which 7 were waited for; matrix products, arithmetic and copies ran while one was open for 6% of the time, Pallas kernels for 0%

commit v1 on v0

v1 whole, which is shorter than its diff:
```python
import jax
import jax.numpy as jnp
from jax import lax
from jax.experimental import pallas as pl
from jax.experimental.pallas import tpu as pltpu
from jax.sharding import PartitionSpec as P

QH = 32
KVH = 4
HD = 128
TOPK = 8
NSEQ = 8
TOK = 64
DOCTOK = 512
CDEV = 512
WIDTH = 2048
LOG2E = 1.4426950408889634
MESH = pl.DeviceIdType.MESH


def attention_kernel(
    len_ref, q_hbm, kn_hbm, vn_hbm, kc_hbm, vc_hbm, w_hbm, res_hbm, mixed_ref,
    qbuf, qext, kbuf, vbuf, acc, mbuf, wbuf, resbuf, part, sib_out, sib_in, x_out, x_in,
    loc_sem, kv_send, kv_recv, fw_send, fw_recv, q_send, q_recv, s_send, s_recv, x_send, x_recv,
):
    me = lax.axis_index("seq")
    ex = lax.axis_index("exp")
    x, c = me // 2, lax.rem(me, 2)
    other = 1 - c
    sibling = (2 * x + other, ex)

    def chip(d):
        return lax.rem(x + d, 4)

    barrier = pltpu.get_barrier_semaphore()
    for d in range(1, NSEQ):
        pl.semaphore_signal(
            barrier, inc=1, device_id=(lax.rem(me + d, NSEQ), ex), device_id_type=MESH
        )
    pl.semaphore_wait(barrier, NSEQ - 1)

    def rows_of(src):
        cached = pl.ds(pl.multiple_of(src * CDEV, CDEV), CDEV)
        fresh = pl.ds(pl.multiple_of(NSEQ * CDEV + src * TOK, TOK), TOK)
        return cached, fresh

    lanes = pl.ds(0, HD)

    def pieces(head, src):
        cols = pl.ds(pl.multiple_of(head * HD, HD), HD)
        cached, fresh = rows_of(src)
        return (
            (kc_hbm.at[:, cols], kbuf.at[cached, lanes]),
            (vc_hbm.at[:, cols], vbuf.at[cached, lanes]),
            (kn_hbm.at[:, cols], kbuf.at[fresh, lanes]),
            (vn_hbm.at[:, cols], vbuf.at[fresh, lanes]),
        )

    q_copies = []
    for d in (1, 2, 3, 5, 6, 7, 4):
        to = lax.rem(me + d, NSEQ)
        q_copies.append(pltpu.make_async_remote_copy(
            src_ref=q_hbm.at[:, pl.ds(pl.multiple_of(to * 512, 512), 512)],
            dst_ref=qbuf.at[pl.ds(pl.multiple_of(me * TOK, TOK), TOK), :],
            send_sem=q_send.at[d], recv_sem=q_recv.at[d],
            device_id=(to, ex), device_id_type=MESH,
        ))
    kv_copies = {}
    for d in (1, 3, 2):
        kv_copies[d] = [
            pltpu.make_async_remote_copy(
                src_ref=src, dst_ref=dst, send_sem=kv_send.at[d, i], recv_sem=kv_recv.at[d, i],
                device_id=(2 * chip(d) + c, ex), device_id_type=MESH,
            )
            for i, (src, dst) in enumerate(pieces(chip(d), me))
        ]
    fw_copies = {0: [
        pltpu.make_async_remote_copy(
            src_ref=src, dst_ref=dst, send_sem=fw_send.at[0, i], recv_sem=fw_recv.at[0, i],
            device_id=sibling, device_id_type=MESH,
        )
        for i, (src, dst) in enumerate(pieces(x, me))
    ]}
    local = [
        pltpu.make_async_copy(src, dst, loc_sem.at[i])
        for i, (src, dst) in enumerate(pieces(x, me))
    ]
    local.append(pltpu.make_async_copy(
        q_hbm.at[:, pl.ds(pl.multiple_of(me * 512, 512), 512)],
        qbuf.at[pl.ds(pl.multiple_of(me * TOK, TOK), TOK), :], loc_sem.at[4]))
    local.append(pltpu.make_async_copy(w_hbm, wbuf, loc_sem.at[5]))
    local.append(pltpu.make_async_copy(res_hbm, resbuf, loc_sem.at[6]))

    for cp in q_copies:
        cp.start()
    for cp in fw_copies[0]:
        cp.start()
    for cp in kv_copies[1] + kv_copies[3] + kv_copies[2]:
        cp.start()
    for cp in local:
        cp.start()

    total = NSEQ * (CDEV + TOK)
    upper = pl.ds(HD, HD)
    lane = lax.broadcasted_iota(jnp.int32, (total, HD), 1)
    pos = lax.broadcasted_iota(jnp.int32, (total, HD), 0)
    hidden = (pos >= len_ref[0]) & (pos < NSEQ * CDEV) & (lane == 0)
    kbuf[:, HD:] = jnp.where(hidden, jnp.float32(-1e30), jnp.float32(0.0)).astype(jnp.bfloat16)
    vbuf[:, HD:] = jnp.ones((total, HD), jnp.bfloat16)
    acc[...] = jnp.zeros_like(acc)
    mbuf[...] = jnp.full(mbuf.shape, -3e38, jnp.float32)

    for cp in q_copies:
        cp.wait_recv()
    local[4].wait()
    unit = (lax.broadcasted_iota(jnp.int32, (DOCTOK, HD), 1) == 0).astype(jnp.float32)
    for h in range(4):
        qext[h, :, :HD] = qbuf[:, h * HD:(h + 1) * HD]
        qext[h, :, HD:] = unit.astype(jnp.bfloat16)

    factor = jnp.float32(LOG2E / (HD ** 0.5))

    def attend(first, count, causal):
        keys_at = pl.ds(first, count)

        def one_head(h, carry):
            for half in range(2):
                rows = pl.ds(half * 256, 256)
                s = lax.dot_general(
                    qext[h, rows, :], kbuf[keys_at, :], (((1,), (1,)), ((), ())),
                    preferred_element_type=jnp.float32,
                )
                if causal:
                    t = lax.broadcasted_iota(jnp.int32, s.shape, 0) + half * 256
                    u = lax.broadcasted_iota(jnp.int32, s.shape, 1)
                    s = jnp.where(u <= t, s, jnp.float32(-1e30))
                m_old = mbuf[h, rows, :]
                m_new = jnp.maximum(m_old, jnp.max(s, axis=1, keepdims=True))
                mbuf[h, rows, :] = m_new
                alpha = jnp.exp2((m_old - m_new) * factor)
                p = jnp.exp2((s - m_new[:, :1]) * factor).astype(jnp.bfloat16)
                pv = jnp.dot(p, vbuf[keys_at, :], preferred_element_type=jnp.float32)
                acc[h, rows, :HD] = acc[h, rows, :HD] * alpha + pv[:, :HD]
                acc[h, rows, HD:] = acc[h, rows, HD:] * alpha + pv[:, HD:]
            return carry

        lax.fori_loop(0, 4, one_head, 0)

    for i in range(4):
        local[i].wait()
    for cp in fw_copies[0]:
        cp.wait_recv()
    attend(pl.multiple_of(x * 1024, 1024), 1024, False)
    for d in (1, 3, 2):
        for cp in kv_copies[d]:
            cp.wait_recv()
        src = 2 * lax.rem(x + 4 - d, 4) + c
        cached, fresh = rows_of(src)
        views = (kbuf.at[cached, lanes], vbuf.at[cached, lanes],
                 kbuf.at[fresh, lanes], vbuf.at[fresh, lanes])
        fw_copies[d] = [
            pltpu.make_async_remote_copy(
                src_ref=view, dst_ref=view, send_sem=fw_send.at[d, i], recv_sem=fw_recv.at[d, i],
                device_id=sibling, device_id_type=MESH,
            )
            for i, view in enumerate(views)
        ]
        for cp in fw_copies[d]:
            cp.start()
        for cp in fw_copies[d]:
            cp.wait_recv()
        attend(pl.multiple_of(lax.rem(x + 4 - d, 4) * 1024, 1024), 1024, False)
    attend(NSEQ * CDEV, DOCTOK, True)

    for h in range(4):
        qbuf[:, h * HD:(h + 1) * HD] = (acc[h, :, :HD] / acc[h, :, HD:]).astype(jnp.bfloat16)
    local[5].wait()

    sib_copies, x_copies = [], []
    for d in (2, 1, 3, 0):
        to = chip(d)
        theirs = pl.ds(pl.multiple_of((2 * to + other) * TOK, TOK), TOK)
        mine = pl.ds(pl.multiple_of((2 * to + c) * TOK, TOK), TOK)
        sib_out[d] = jnp.dot(
            qbuf[theirs, :], wbuf[...], preferred_element_type=jnp.float32
        ).astype(jnp.bfloat16)
        cp = pltpu.make_async_remote_copy(
            src_ref=sib_out.at[d], dst_ref=sib_in.at[d], send_sem=s_send.at[d],
            recv_sem=s_recv.at[d], device_id=sibling, device_id_type=MESH,
        )
        cp.start()
        sib_copies.append((d, cp))
        part[d] = jnp.dot(qbuf[mine, :], wbuf[...], preferred_element_type=jnp.float32)
    for d, cp in sib_copies:
        cp.wait_recv()
        if d:
            x_out[d] = (part[d] + sib_in[d].astype(jnp.float32)).astype(jnp.bfloat16)
            xcp = pltpu.make_async_remote_copy(
                src_ref=x_out.at[d], dst_ref=x_in.at[d], send_sem=x_send.at[d],
                recv_sem=x_recv.at[d], device_id=(2 * chip(d) + c, ex), device_id_type=MESH,
            )
            xcp.start()
            x_copies.append(xcp)
    local[6].wait()
    total_sum = resbuf[...].astype(jnp.float32) + part[0] + sib_in[0].astype(jnp.float32)
    for xcp in x_copies:
        xcp.wait_recv()
    for d in (1, 2, 3):
        total_sum = total_sum + x_in[d].astype(jnp.float32)
    mixed_ref[...] = total_sum

    for cp in q_copies + x_copies + [cp for _, cp in sib_copies]:
        cp.wait_send()
    for d in (0, 1, 2, 3):
        for cp in fw_copies[d]:
            cp.wait_send()
        if d:
            for cp in kv_copies[d]:
                cp.wait_send()


def attention_mixed(queries, new_keys, new_values, cache_keys, cache_values, cache_len, residual, out_weight):
    anyspec = pl.BlockSpec(memory_space=pl.ANY)
    total = NSEQ * (CDEV + TOK)
    bf, f32 = jnp.bfloat16, jnp.float32
    dma = pltpu.SemaphoreType.DMA
    return pl.pallas_call(
        attention_kernel,
        out_shape=jax.ShapeDtypeStruct((TOK, WIDTH), f32),
        in_specs=[pl.BlockSpec(memory_space=pltpu.SMEM)] + [anyspec] * 7,
        out_specs=pl.BlockSpec(memory_space=pltpu.VMEM),
        scratch_shapes=[
            pltpu.VMEM((DOCTOK, 512), bf),
            pltpu.VMEM((4, DOCTOK, 256), bf),
            pltpu.VMEM((total, 256), bf),
            pltpu.VMEM((total, 256), bf),
            pltpu.VMEM((4, DOCTOK, 256), f32),
            pltpu.VMEM((4, DOCTOK, HD), f32),
            pltpu.VMEM((512, WIDTH), bf),
            pltpu.VMEM((TOK, WIDTH), bf),
            pltpu.VMEM((4, TOK, WIDTH), f32),
            pltpu.VMEM((4, TOK, WIDTH), bf),
            pltpu.VMEM((4, TOK, WIDTH), bf),
            pltpu.VMEM((4, TOK, WIDTH), bf),
            pltpu.VMEM((4, TOK, WIDTH), bf),
            dma((7,)), dma((4, 4)), dma((4, 4)), dma((4, 4)), dma((4, 4)),
            dma((8,)), dma((8,)), dma((4,)), dma((4,)), dma((4,)), dma((4,)),
        ],
        compiler_params=pltpu.CompilerParams(
            collective_id=0, has_side_effects=True, vmem_limit_bytes=56 * 2**20
        ),
        name="attention_exchange",
    )(cache_len, queries[0], new_keys[0], new_values[0], cache_keys[0], cache_values[0],
      out_weight, residual[0])


def expert_token_rows(piece, gate_proj, up_proj, down_proj):
    width = piece.shape[-1]
    rows = piece.reshape(-1, width)
    gate = jnp.dot(rows, gate_proj[0], preferred_element_type=jnp.float32)
    upv = jnp.dot(rows, up_proj[0], preferred_element_type=jnp.float32)
    act = (jax.nn.silu(gate) * upv).astype(jnp.bfloat16)
    result = jnp.dot(act, down_proj[0], preferred_element_type=jnp.float32).astype(jnp.bfloat16)
    return result.reshape(piece.shape)


def body(
    queries,
    new_keys,
    new_values,
    cache_keys,
    cache_values,
    cache_len,
    residual_in,
    out_weight,
    norm_gain,
    router_weight,
    expert_ids,
    gate_proj,
    up_proj,
    down_proj,
):
    tokens = queries.shape[1]
    width = residual_in.shape[2]
    mixed = attention_mixed(
        queries, new_keys, new_values, cache_keys, cache_values, cache_len, residual_in, out_weight
    )
    meansq = jnp.mean(mixed * mixed, axis=-1, keepdims=True)
    normed = (mixed / jnp.sqrt(meansq + 1e-06) * norm_gain).astype(jnp.bfloat16)
    logits = jnp.dot(normed, router_weight, preferred_element_type=jnp.float32)
    nexp = router_weight.shape[1]
    chosen = expert_ids[0]
    onehot = chosen[:, :, None] == jnp.arange(nexp, dtype=jnp.int32)[None, None, :]
    picked = jnp.sum(jnp.where(onehot, logits[:, None, :], jnp.float32(0.0)), axis=2)
    expo = jnp.exp(picked)
    gates = expo / jnp.sum(expo, axis=1, keepdims=True)
    capacity = 3 * tokens * TOPK // (2 * nexp)
    flat = chosen.reshape(-1)
    member = (flat[:, None] == jnp.arange(nexp, dtype=jnp.int32)[None, :]).astype(jnp.int32)
    rank = jnp.sum((jnp.cumsum(member, axis=0) - 1) * member, axis=1)
    slot = flat * capacity + rank
    place = slot[:, None] == jnp.arange(nexp * capacity, dtype=jnp.int32)[None, :]
    route = jnp.any(place.reshape(tokens, TOPK, nexp * capacity), axis=1).astype(jnp.bfloat16)
    packed = jnp.einsum("ts,td->sd", route, normed, preferred_element_type=jnp.float32).astype(
        jnp.bfloat16
    )
    outgoing = packed.reshape(nexp, capacity, width)
    result = expert_token_rows(
        lax.all_to_all(outgoing, ("seq", "exp"), split_axis=0, concat_axis=0, tiled=True),
        gate_proj,
        up_proj,
        down_proj,
    )
    back = lax.all_to_all(result, ("seq", "exp"), split_axis=0, concat_axis=0, tiled=True)
    back = back.reshape(nexp * capacity, width)
    gathered = back[slot].reshape(tokens, TOPK, width)
    moe = jnp.sum(gates[:, :, None] * gathered.astype(jnp.float32), axis=1)
    return (mixed + moe).astype(jnp.bfloat16).reshape(1, tokens, width)


def solution(mesh):
    in_specs = (
        P("exp", "seq", None),
        P("exp", "seq", None),
        P("exp", "seq", None),
        P("exp", "seq", None),
        P("exp", "seq", None),
        P("exp"),
        P("exp", "seq", None),
        P("seq", None),
        P(),
        P(),
        P("exp", "seq", None),
        P(("seq", "exp"), None, None),
        P(("seq", "exp"), None, None),
        P(("seq", "exp"), None, None),
    )
    out_specs = P("exp", "seq", None)
    return jax.shard_map(body, mesh=mesh, in_specs=in_specs, out_specs=out_specs, check_vma=False)
```

time: 374 us -> 246 us (0.66)
  waiting for transfers between devices: 112 us -> 50 us
  Pallas kernels: 0 us -> 60.9 us
  matrix products: 63.6 us -> 21.9 us
  starting transfers between devices: 31.2 us -> 6.22 us
  other arithmetic: 32 us -> 9.13 us
  local copies, waits for them, and re-layouts: 55.6 us -> 34.2 us
  between operations: 14.2 us -> 0.83 us
    pallas_call x0 -> x1, Pallas kernels: none -> 60.9 us  [attention_mixed(): pl.pallas_call(attention_kernel, out_shape=jax.ShapeDtypeStruct((TOK, WID...]
    dot_general x3 -> x0, matrix products: 41.5 us -> none  [the longest x1 18.9 us: attend(): jnp.einsum('pgbk,kpd->bpgd', weight_matrices, value_entries, preferred_el...]
    reduce_scatter x1 -> x0, waiting for transfers between devices: 32.1 us -> none  [body(): lax.psum_scatter(jnp.dot(attn, out_weight, preferred_element_type=jnp.flo...]
    all_to_all x5 -> x0, waiting for transfers between devices: 30.3 us -> none  [the longest x1 10.6 us: attention_per_head(): lax.all_to_all(spread_heads(cache_values[0], nseq), 'seq', split_axis=1,...]
    all_to_all x5 -> x0, starting transfers between devices: 25 us -> none  [the longest x1 5.79 us: attention_per_head(): lax.all_to_all(spread_heads(new_keys[0], nseq), 'seq', split_axis=1, conc...]
    reduce_sum x1 -> x0, other arithmetic: 16.1 us -> none  [attend(): jnp.sum(expo, axis=-1, keepdims=True)]
    broadcast_in_dim x11 -> x0, local copies, waits for them, and re-layouts: 13.6 us -> none  [spread_heads(): heads = jnp.broadcast_to(heads, (count, KVH, repeat, HD))]
    select_n x1 -> x0, other arithmetic: 5.77 us -> none  [attend(): visible = jnp.where(kpos < ncache, kpos < length, kpos - ncache <= qpos)]
  transfers between devices with their start and end apart: 7 -> 1, of which waited for: 7 -> 1; matrix products, arithmetic and copies ran while one was open for 6% -> 1% of each run, Pallas kernels for 0% -> 0%
where the time goes in v1:
time: 246 us; the launch traced here: 245 us
  blocking collectives  61.9 us (25%)
  Pallas kernels  60.9 us (25%)
  waiting for transfers between devices  50 us (20%)
  local copies, waits for them, and re-layouts  34.2 us (14%)
  matrix products  21.9 us (9%)
  other arithmetic  9.13 us (4%)
  starting transfers between devices  6.22 us (3%)
    all_to_all x1, blocking collectives, body(): lax.all_to_all(outgoing, ('seq', 'exp'), split_axis=0, concat_axis=0, til...  61.9 us
    pallas_call x1, Pallas kernels, attention_mixed(): pl.pallas_call(attention_kernel, out_shape=jax.ShapeDtypeStruct((TOK, WID...  60.9 us
    all_to_all x1, waiting for transfers between devices, body(): lax.all_to_all(result, ('seq', 'exp'), split_axis=0, concat_axis=0, tiled...  50 us
    dot_general x1, matrix products, expert_token_rows(): jnp.dot(act, down_proj[0], preferred_element_type=jnp.float32)  11 us
    gather x1, local copies, waits for them, and re-layouts, body(): gathered = back[slot].reshape(tokens, TOPK, width)  7.51 us
    dot_general x1, matrix products, expert_token_rows(): upv = jnp.dot(rows, up_proj[0], preferred_element_type=jnp.float32)  6.92 us
    reshape x1, local copies, waits for them, and re-layouts, body(): back = back.reshape(nexp * capacity, width)  6.32 us
    reshape x1, local copies, waits for them, and re-layouts, expert_token_rows(): rows = piece.reshape(-1, width)  6.32 us
  transfers between devices with their start and end apart: 1, of which 1 were waited for; matrix products, arithmetic and copies ran while one was open for 1% of the time, Pallas kernels for 0%

profile of v1, /device:TPU:1, one launch (start us, length us, event | category | flops | bytes accessed | tf_op | source)
XLA Modules:
  0.0 245.0 jit_solution(11443690253202261053)
XLA Ops:
  0.0 0.0 copy-start
  0.0 0.9 copy.23
  0.9 0.1 eq.62
  1.0 0.1 eq.58
  1.8 0.1 copy.26
  1.9 0.2 fusion.13
  2.1 0.1 add_add_fusion
  2.2 0.0 copy-start.2
  2.2 0.2 fusion.12
  2.5 0.1 reduce_sum.53
  2.6 0.5 fusion.8
  3.1 60.9 %attention_exchange.1 = f32[64,2048]{1,0:T(8,128)} custom-call(s32[1]{0:T(128)S(6)} %copy.29.len_ref, bf16[64,4096]{1,0:T(8,128)(2,1)} %bitcast.43, bf16[64,512]{1,0:T(8,128)(2,1)} %bitcast.47, bf16[64,512]{1,0:T(8,128)(2,1)} %bitcast.48, bf16[512,512]{1,0:T(8,128)(2,1)} %bitcast.44, bf16[512,512]{1,0:T(8,128)(2,1)} %bitcast.45, bf16[512,2048]{1,0:T(8,128)(2,1)} %w_hbm.1, ...), custom_call_target="tpu_custom_call" | custom-call | tf_op jit(solution)/shard_map/attention_exchange/pallas_call | solution.py:227
  64.0 1.2 multiply_reduce_fusion
  65.2 0.0 copy-done.2
  65.2 1.2 multiply_convert_fusion.1
  66.4 2.7 %convolution_convert_fusion.1 = bf16[768,2048]{1,0:T(8,128)(2,1)} fusion(pred[64,768]{1,0:T(8,128)(4,1)S(1)} %fusion.8, bf16[64,2048]{1,0:T(8,128)(2,1)S(1)} %multiply_convert_fusion.1), kind=kOutput, calls=%fused_computation.4 | convolution fusion | flops 202899456 | bytes 3457024 | tf_op jit(solution)/shard_map/ts,td->sd/dot_general | solution.py:304
  69.1 6.2 %reshape.111 = bf16[128,6,2048]{2,1,0:T(8,128)(2,1)} reshape(bf16[768,2048]{1,0:T(8,128)(2,1)} %convolution_convert_fusion.1) | data formatting | bytes 6291456 | tf_op jit(solution)/shard_map/reshape | solution.py:307
  75.3 61.9 %all_to_all.10 = bf16[128,6,2048]{2,1,0:T(8,128)(2,1)} all-to-all(bf16[128,6,2048]{2,1,0:T(8,128)(2,1)} %reshape.111), channel_id=1, replica_groups=mesh['seq'=8,'exp'=16] {'seq','exp'}, dimensions={0} | all-to-all | bytes 6291456 | tf_op jit(solution)/shard_map/all_to_all | solution.py:309
  137.2 6.3 %reshape.112 = bf16[768,2048]{1,0:T(8,128)(2,1)} reshape(bf16[128,6,2048]{2,1,0:T(8,128)(2,1)} %all_to_all.10) | data formatting | bytes 6291456 | tf_op jit(solution)/shard_map/reshape | solution.py:259
  143.5 6.9 %fusion.2 = f32[768,768]{1,0:T(8,128)} fusion(bf16[768,2048]{1,0:T(8,128)(2,1)} %reshape.112, bf16[1,2048,768]{2,1,0:T(8,128)(2,1)} %param.26), kind=kOutput, calls=%fused_computation.6 | convolution fusion | flops 2415919104 | bytes 8650752 | tf_op jit(solution)/shard_map/dot_general | solution.py:261
  150.4 0.0 copy-done
  150.4 11.0 %convolution_convert_fusion = bf16[768,2048]{1,0:T(8,128)(2,1)} fusion(bf16[1,768,2048]{2,1,0:T(8,128)(2,1)S(1)} %copy-done, f32[768,768]{1,0:T(8,128)} %fusion.2, bf16[768,2048]{1,0:T(8,128)(2,1)} %reshape.112, bf16[1,2048,768]{2,1,0:T(8,128)(2,1)} %param.25), kind=kOutput, calls=%fused_computation.3 | convolution fusion | flops 4836950016 | bytes 14942208 | tf_op jit(solution)/shard_map/dot_general | solution.py:263
  161.5 6.3 %reshape.113 = bf16[128,6,2048]{2,1,0:T(8,128)(2,1)} reshape(bf16[768,2048]{1,0:T(8,128)(2,1)} %convolution_convert_fusion) | data formatting | bytes 6291456 | tf_op jit(solution)/shard_map/reshape | solution.py:264
  167.7 0.0 copy-start.1
  167.7 6.2 %all-to-all-start.1 = ((bf16[128,6,2048]{2,1,0:T(8,128)(2,1)}), bf16[128,6,2048]{2,1,0:T(8,128)(2,1)}, u32[]{:S(2)}, u32[]{:S(2)}) async-start(bf16[128,6,2048]{2,1,0:T(8,128)(2,1)} %reshape.113), calls=%async_computation.1 | async-start | bytes 8388608 | tf_op jit(solution)/shard_map/all_to_all | solution.py:314
  173.9 0.0 copy-done.1
  174.0 0.1 copy.28
  174.1 0.1 mul.63
  174.2 1.3 fusion.17
  175.4 0.2 select_reduce_fusion
  175.7 0.1 exponential_reduce_fusion
  175.8 0.1 exponential_divide_fusion
  175.9 50.0 %all-to-all-done.1 = bf16[128,6,2048]{2,1,0:T(8,128)(2,1)} async-done(((bf16[128,6,2048]{2,1,0:T(8,128)(2,1)}), bf16[128,6,2048]{2,1,0:T(8,128)(2,1)}, u32[]{:S(2)}, u32[]{:S(2)}) %all-to-all-start.1) | async-done | bytes 3145760 | tf_op jit(solution)/shard_map/all_to_all | solution.py:314
  225.9 6.3 %reshape.114 = bf16[768,2048]{1,0:T(8,128)(2,1)} reshape(bf16[128,6,2048]{2,1,0:T(8,128)(2,1)} %all-to-all-done.1) | data formatting | bytes 6291456 | tf_op jit(solution)/shard_map/reshape | solution.py:315
  232.2 7.5 %gather_fusion = bf16[512,2048]{1,0:T(8,128)(2,1)} fusion(bf16[768,2048]{1,0:T(8,128)(2,1)} %reshape.114, s32[1024]{0:T(1024)S(1)} %pad_clamp_fusion), kind=kCustom, calls=%fused_computation | custom fusion | bytes 4196352 | tf_op jit(solution)/shard_map/gather | solution.py:316
  239.7 3.4 %fusion = f32[64,2048]{1,0:T(8,128)S(1)} fusion(bf16[512,2048]{1,0:T(8,128)(2,1)} %gather_fusion, f32[64,8]{1,0:T(8,128)S(1)} %exponential_divide_fusion), kind=kLoop, calls=%fused_computation.2 | loop fusion | flops 3014656 | bytes 2623488 | tf_op jit(solution)/shard_map/reduce_sum | solution.py:317
  243.2 1.8 fusion.11
  (9 shorter events, 0.1 us)
Async XLA Ops:
  0.0 150.4 %copy-start = (bf16[1,768,2048]{2,1,0:T(8,128)(2,1)S(1)}, bf16[1,768,2048]{2,1,0:T(8,128)(2,1)}, u32[]{:S(2)}) copy-start(bf16[1,768,2048]{2,1,0:T(8,128)(2,1)} %param.27) | copy-start | bytes 9437188
  2.2 63.0 %copy-start.2 = (f32[2048]{0:T(1024)S(1)}, f32[2048]{0:T(1024)}, u32[]{:S(2)}) copy-start(f32[2048]{0:T(1024)} %param.22) | copy-start | bytes 24580
  167.7 6.2 %copy-start.1 = (s32[1,64,8]{1,2,0:T(8,128)S(1)}, s32[1,64,8]{1,2,0:T(8,128)}, u32[]{:S(2)}) copy-start(s32[1,64,8]{1,2,0:T(8,128)} %param.24) | copy-start | bytes 6148
  167.7 58.2 %all-to-all-start.1 = ((bf16[128,6,2048]{2,1,0:T(8,128)(2,1)}), bf16[128,6,2048]{2,1,0:T(8,128)(2,1)}, u32[]{:S(2)}, u32[]{:S(2)}) async-start(bf16[128,6,2048]{2,1,0:T(8,128)(2,1)} %reshape.113), calls=%async_computation.1 | async-start | bytes 8388608 | tf_op jit(solution)/shard_map/all_to_all | solution.py:314

commit v2 on v1

--- a/solution.py
+++ b/solution.py
@@ -254,68 +254,307 @@
       out_weight, residual[0])
 
 
-def expert_token_rows(piece, gate_proj, up_proj, down_proj):
-    width = piece.shape[-1]
-    rows = piece.reshape(-1, width)
-    gate = jnp.dot(rows, gate_proj[0], preferred_element_type=jnp.float32)
-    upv = jnp.dot(rows, up_proj[0], preferred_element_type=jnp.float32)
-    act = (jax.nn.silu(gate) * upv).astype(jnp.bfloat16)
-    result = jnp.dot(act, down_proj[0], preferred_element_type=jnp.float32).astype(jnp.bfloat16)
-    return result.reshape(piece.shape)
+EXPERTS = 128
+FF = 768
+PEERS = 16
+SLOTS = 48
+CAP = 6
+ROWS = PEERS * SLOTS
+NCHUNK = 4
+CHUNK = WIDTH // NCHUNK
+
+
+def experts_kernel(
+    mixed_hbm, gain_ref, router_ref, ids_ref, wg_hbm, wu_hbm, wd_hbm, out_ref,
+    mixed, tokens, table, pick, give, outbox, inbox, wg, wu, wd, hg, hu, act,
+    results, back, part, sib_out, sib_in, x_out, x_in,
+    loc_sem, t_send, t_recv, a_send, a_recv, f_send, f_recv, d_send, d_recv, r_send, r_recv,
+    s_send, s_recv, x_send, x_recv,
+):
+    me = lax.axis_index("seq")
+    ex = lax.axis_index("exp")
+    x, c = me // 2, lax.rem(me, 2)
+    other = 1 - c
+    sibling = (2 * x + other, ex)
+    f32, bf = jnp.float32, jnp.bfloat16
+
+    def chip(d):
+        return lax.rem(x + d, 4)
+
+    def peer(d):
+        return (me, plane_index(ex, d))
+
+    loads = [
+        pltpu.make_async_copy(mixed_hbm, mixed, loc_sem.at[0]),
+        pltpu.make_async_copy(wg_hbm, wg, loc_sem.at[1]),
+        pltpu.make_async_copy(wu_hbm, wu, loc_sem.at[2]),
+        pltpu.make_async_copy(wd_hbm, wd, loc_sem.at[3]),
+    ]
+    for cp in loads:
+        cp.start()
+    barrier = pltpu.get_barrier_semaphore()
+    for d in range(1, NSEQ):
+        pl.semaphore_signal(
+            barrier, inc=1, device_id=(lax.rem(me + d, NSEQ), ex), device_id_type=MESH
+        )
+    for d in range(1, PEERS):
+        pl.semaphore_signal(barrier, inc=1, device_id=peer(d), device_id_type=MESH)
+    loads[0].wait()
+
+    def block(s):
+        return pl.ds(pl.multiple_of(s * TOK, TOK), TOK)
+
+    def group(e):
+        return pl.ds(pl.multiple_of(e * SLOTS, 16), SLOTS)
+
+    def span(k):
+        return pl.ds(k * CHUNK, CHUNK)
+
+    mx = mixed[...]
+    meansq = jnp.mean(mx * mx, axis=1, keepdims=True)
+    normed = (mx / jnp.sqrt(meansq + 1e-06) * gain_ref[...]).astype(bf)
+    tokens[block(me), :] = normed
+    pl.semaphore_wait(barrier, NSEQ - 1 + PEERS - 1)
+
+    a_copies = {}
+    for k in range(NCHUNK):
+        for d in (0, 2, 1, 3):
+            to = sibling if d == 0 else (2 * chip(d) + c, ex)
+            view = tokens.at[block(me), span(k)]
+            cp = pltpu.make_async_remote_copy(
+                src_ref=view, dst_ref=view, send_sem=a_send.at[k, d], recv_sem=a_recv.at[k, d],
+                device_id=to, device_id_type=MESH,
+            )
+            cp.start()
+            a_copies[k, d] = cp
+
+    logits = jnp.dot(normed, router_ref[...], preferred_element_type=f32)
+    lane = lax.broadcasted_iota(jnp.int32, (TOK, EXPERTS), 1)
+    chosen = jnp.zeros((TOK, EXPERTS), f32)
+    for k in range(TOPK):
+        chosen = chosen + jnp.where(ids_ref[:, k:k + 1] == lane, f32(1.0), f32(0.0))
+    expo = jnp.where(chosen > 0, jnp.exp(logits), f32(0.0))
+    gates = expo / jnp.sum(expo, axis=1, keepdims=True)
+    before = (lax.broadcasted_iota(jnp.int32, (TOK, TOK), 1)
+              < lax.broadcasted_iota(jnp.int32, (TOK, TOK), 0)).astype(f32)
+    rank = jnp.dot(before.astype(bf), chosen.astype(bf), preferred_element_type=f32)
+    first = (CAP * me + 1).astype(f32)
+    place = jnp.where(chosen > 0, rank + first, f32(0.0))
+    table[block(me), :EXPERTS] = place.astype(bf)
+    table[block(me), EXPERTS:] = gates.astype(bf)
+    t_copies = []
+    for d in range(1, NSEQ):
+        view = table.at[block(me), :]
+        cp = pltpu.make_async_remote_copy(
+            src_ref=view, dst_ref=view, send_sem=t_send.at[d], recv_sem=t_recv.at[d],
+            device_id=(lax.rem(me + d, NSEQ), ex), device_id_type=MESH,
+        )
+        cp.start()
+        t_copies.append(cp)
+
+    f_copies = {}
+
+    def forward(k):
+        for d in (2, 1, 3):
+            a_copies[k, d].wait_recv()
+            view = tokens.at[block(2 * lax.rem(x + 4 - d, 4) + c), span(k)]
+            cp = pltpu.make_async_remote_copy(
+                src_ref=view, dst_ref=view, send_sem=f_send.at[k, d], recv_sem=f_recv.at[k, d],
+                device_id=sibling, device_id_type=MESH,
+            )
+            cp.start()
+            f_copies[k, d] = cp
+
+    for cp in t_copies:
+        cp.wait_recv()
+    qi = lax.broadcasted_iota(jnp.int32, (ROWS, EXPERTS), 0)
+    ei = (lax.broadcasted_iota(jnp.int32, (ROWS, EXPERTS), 1) - me * PEERS) * SLOTS
+    owner = jnp.where((qi >= ei) & (qi < ei + SLOTS), f32(1.0), f32(0.0)).astype(bf)
+    nt = (((1,), (1,)), ((), ()))
+
+    def within(shape, axis):
+        at = lax.broadcasted_iota(jnp.int32, shape, axis)
+        low = at + 1
+        for e in range(1, PEERS):
+            low = jnp.where(at >= e * SLOTS, at + 1 - e * SLOTS, low)
+        return low.astype(f32)
+
+    codes, shares = table[:, :EXPERTS], table[:, EXPERTS:]
+    by_row = lax.dot_general(owner, codes, nt, preferred_element_type=f32)
+    pick[...] = jnp.where(by_row == within((ROWS, 128), 0)[:, :1], f32(1.0), f32(0.0)).astype(bf)
+    by_token = lax.dot_general(codes, owner, nt, preferred_element_type=f32)
+    spread = lax.dot_general(shares, owner, nt, preferred_element_type=f32)
+    give[...] = jnp.where(by_token == within((8, ROWS), 1)[:1, :], spread, f32(0.0)).astype(bf)
+
+    d_copies, r_copies = {}, {}
+    for k in range(NCHUNK):
+        forward(k)
+        a_copies[k, 0].wait_recv()
+        for d in (2, 1, 3):
+            f_copies[k, d].wait_recv()
+        outbox[:, span(k)] = jnp.dot(
+            pick[...], tokens[:, span(k)], preferred_element_type=f32
+        ).astype(bf)
+        for d in PLANE_ORDER:
+            to = plane_index(ex, d)
+            cp = pltpu.make_async_remote_copy(
+                src_ref=outbox.at[group(to), span(k)], dst_ref=inbox.at[group(ex), span(k)],
+                send_sem=d_send.at[k, d], recv_sem=d_recv.at[k, d],
+                device_id=(me, to), device_id_type=MESH,
+            )
+            cp.start()
+            d_copies[k, d] = cp
+        inbox[group(ex), span(k)] = outbox[group(ex), span(k)]
+
+    loads[1].wait()
+    loads[2].wait()
+    for k in range(NCHUNK):
+        for d in PLANE_ORDER:
+            d_copies[k, d].wait_recv()
+        rows = inbox[:, span(k)]
+        g = jnp.dot(rows, wg[span(k), :], preferred_element_type=f32)
+        u = jnp.dot(rows, wu[span(k), :], preferred_element_type=f32)
+        if k == 0:
+            hg[...] = g
+            hu[...] = u
+        elif k < NCHUNK - 1:
+            hg[...] += g
+            hu[...] += u
+        else:
+            g = hg[...] + g
+            u = hu[...] + u
+            act[...] = (g / (f32(1.0) + jnp.exp(-g)) * u).astype(bf)
+    loads[3].wait()
+    for k in range(NCHUNK):
+        results[:, span(k)] = jnp.dot(
+            act[...], wd[:, span(k)], preferred_element_type=f32
+        ).astype(bf)
+        for d in PLANE_ORDER:
+            to = plane_index(ex, d)
+            cp = pltpu.make_async_remote_copy(
+                src_ref=results.at[group(to), span(k)], dst_ref=back.at[group(ex), span(k)],
+                send_sem=r_send.at[k, d], recv_sem=r_recv.at[k, d],
+                device_id=(me, to), device_id_type=MESH,
+            )
+            cp.start()
+            r_copies[k, d] = cp
+        back[group(ex), span(k)] = results[group(ex), span(k)]
+
+    s_copies, x_copies = {}, {}
+
+    def reduce_chips(k):
+        for d in (2, 1, 3, 0):
+            s_copies[k, d].wait_recv()
+            if d:
+                x_out[d, :, span(k)] = (
+                    part[d, :, span(k)] + sib_in[d, :, span(k)].astype(f32)
+                ).astype(bf)
+                cp = pltpu.make_async_remote_copy(
+                    src_ref=x_out.at[d, :, span(k)], dst_ref=x_in.at[d, :, span(k)],
+                    send_sem=x_send.at[k, d], recv_sem=x_recv.at[k, d],
+                    device_id=(2 * chip(d) + c, ex), device_id_type=MESH,
+                )
+                cp.start()
+                x_copies[k, d] = cp
+
+    for k in range(NCHUNK):
+        for d in PLANE_ORDER:
+            r_copies[k, d].wait_recv()
+        for d in (2, 1, 3, 0):
+            to = chip(d)
+            sib_out[d, :, span(k)] = jnp.dot(
+                give[block(2 * to + other), :], back[:, span(k)], preferred_element_type=f32
+            ).astype(bf)
+            cp = pltpu.make_async_remote_copy(
+                src_ref=sib_out.at[d, :, span(k)], dst_ref=sib_in.at[d, :, span(k)],
+                send_sem=s_send.at[k, d], recv_sem=s_recv.at[k, d],
+                device_id=sibling, device_id_type=MESH,
+            )
+            cp.start()
+            s_copies[k, d] = cp
+            part[d, :, span(k)] = jnp.dot(
+                give[block(2 * to + c), :], back[:, span(k)], preferred_element_type=f32
+            )
+        if k:
+            reduce_chips(k - 1)
+    reduce_chips(NCHUNK - 1)
+    for k in range(NCHUNK):
+        total = mixed[:, span(k)] + part[0, :, span(k)] + sib_in[0, :, span(k)].astype(f32)
+        for d in (1, 2, 3):
+            x_copies[k, d].wait_recv()
+        for d in (1, 2, 3):
+            total = total + x_in[d, :, span(k)].astype(f32)
+        out_ref[:, span(k)] = total.astype(bf)
+
+    for group_of in (a_copies, f_copies, d_copies, r_copies, s_copies, x_copies):
+        for cp in group_of.values():
+            cp.wait_send()
+    for cp in t_copies:
+        cp.wait_send()
+
+
+PLANE_ORDER = tuple(range(1, PEERS))
+
+
+def plane_index(ex, d):
+    y, z = ex // 4, lax.rem(ex, 4)
+    return lax.rem(y + d // 4, 4) * 4 + lax.rem(z + d % 4, 4)
+
+
+def experts_layer(mixed, gain, router, ids, gate_proj, up_proj, down_proj):
+    anyspec = pl.BlockSpec(memory_space=pl.ANY)
+    vmem = pl.BlockSpec(memory_space=pltpu.VMEM)
+    bf, f32 = jnp.bfloat16, jnp.float32
+    dma = pltpu.SemaphoreType.DMA
+    return pl.pallas_call(
+        experts_kernel,
+        out_shape=jax.ShapeDtypeStruct((TOK, WIDTH), bf),
+        in_specs=[anyspec, vmem, vmem, vmem, anyspec, anyspec, anyspec],
+        out_specs=vmem,
+        scratch_shapes=[
+            pltpu.VMEM((TOK, WIDTH), f32),
+            pltpu.VMEM((DOCTOK, WIDTH), bf),
+            pltpu.VMEM((DOCTOK, 2 * EXPERTS), bf),
+            pltpu.VMEM((ROWS, DOCTOK), bf),
+            pltpu.VMEM((DOCTOK, ROWS), bf),
+            pltpu.VMEM((ROWS, WIDTH), bf),
+            pltpu.VMEM((ROWS, WIDTH), bf),
+            pltpu.VMEM((WIDTH, FF), bf),
+            pltpu.VMEM((WIDTH, FF), bf),
+            pltpu.VMEM((FF, WIDTH), bf),
+            pltpu.VMEM((ROWS, FF), f32),
+            pltpu.VMEM((ROWS, FF), f32),
+            pltpu.VMEM((ROWS, FF), bf),
+            pltpu.VMEM((ROWS, WIDTH), bf),
+            pltpu.VMEM((ROWS, WIDTH), bf),
+            pltpu.VMEM((4, TOK, WIDTH), f32),
+            pltpu.VMEM((4, TOK, WIDTH), bf),
+            pltpu.VMEM((4, TOK, WIDTH), bf),
+            pltpu.VMEM((4, TOK, WIDTH), bf),
+            pltpu.VMEM((4, TOK, WIDTH), bf),
+            dma((4,)), dma((8,)), dma((8,)),
+            dma((NCHUNK, 4)), dma((NCHUNK, 4)), dma((NCHUNK, 4)), dma((NCHUNK, 4)),
+            dma((NCHUNK, 16)), dma((NCHUNK, 16)), dma((NCHUNK, 16)), dma((NCHUNK, 16)),
+            dma((NCHUNK, 4)), dma((NCHUNK, 4)), dma((NCHUNK, 4)), dma((NCHUNK, 4)),
+        ],
+        compiler_params=pltpu.CompilerParams(
+            collective_id=1, has_side_effects=True, vmem_limit_bytes=60 * 2**20
+        ),
+        name="experts_exchange",
+    )(mixed, gain.reshape(1, WIDTH), router, ids, gate_proj[0], up_proj[0], down_proj[0])
 
 
 def body(
-    queries,
-    new_keys,
-    new_values,
-    cache_keys,
-    cache_values,
-    cache_len,
-    residual_in,
-    out_weight,
-    norm_gain,
-    router_weight,
-    expert_ids,
-    gate_proj,
-    up_proj,
-    down_proj,
+    queries, new_keys, new_values, cache_keys, cache_values, cache_len, residual_in,
+    out_weight, norm_gain, router_weight, expert_ids, gate_proj, up_proj, down_proj,
 ):
-    tokens = queries.shape[1]
-    width = residual_in.shape[2]
     mixed = attention_mixed(
         queries, new_keys, new_values, cache_keys, cache_values, cache_len, residual_in, out_weight
     )
-    meansq = jnp.mean(mixed * mixed, axis=-1, keepdims=True)
-    normed = (mixed / jnp.sqrt(meansq + 1e-06) * norm_gain).astype(jnp.bfloat16)
-    logits = jnp.dot(normed, router_weight, preferred_element_type=jnp.float32)
-    nexp = router_weight.shape[1]
-    chosen = expert_ids[0]
-    onehot = chosen[:, :, None] == jnp.arange(nexp, dtype=jnp.int32)[None, None, :]
-    picked = jnp.sum(jnp.where(onehot, logits[:, None, :], jnp.float32(0.0)), axis=2)
-    expo = jnp.exp(picked)
-    gates = expo / jnp.sum(expo, axis=1, keepdims=True)
-    capacity = 3 * tokens * TOPK // (2 * nexp)
-    flat = chosen.reshape(-1)
-    member = (flat[:, None] == jnp.arange(nexp, dtype=jnp.int32)[None, :]).astype(jnp.int32)
-    rank = jnp.sum((jnp.cumsum(member, axis=0) - 1) * member, axis=1)
-    slot = flat * capacity + rank
-    place = slot[:, None] == jnp.arange(nexp * capacity, dtype=jnp.int32)[None, :]
-    route = jnp.any(place.reshape(tokens, TOPK, nexp * capacity), axis=1).astype(jnp.bfloat16)
-    packed = jnp.einsum("ts,td->sd", route, normed, preferred_element_type=jnp.float32).astype(
-        jnp.bfloat16
+    out = experts_layer(
+        mixed, norm_gain, router_weight, expert_ids[0], gate_proj, up_proj, down_proj
     )
-    outgoing = packed.reshape(nexp, capacity, width)
-    result = expert_token_rows(
-        lax.all_to_all(outgoing, ("seq", "exp"), split_axis=0, concat_axis=0, tiled=True),
-        gate_proj,
-        up_proj,
-        down_proj,
-    )
-    back = lax.all_to_all(result, ("seq", "exp"), split_axis=0, concat_axis=0, tiled=True)
-    back = back.reshape(nexp * capacity, width)
-    gathered = back[slot].reshape(tokens, TOPK, width)
-    moe = jnp.sum(gates[:, :, None] * gathered.astype(jnp.float32), axis=1)
-    return (mixed + moe).astype(jnp.bfloat16).reshape(1, tokens, width)
+    return out.reshape(1, TOK, WIDTH)
 
 
 def solution(mesh):

time: 246 us -> 183 us (0.74)
  Pallas kernels: 60.9 us -> 178 us
  blocking collectives: 61.9 us -> 0 us
  waiting for transfers between devices: 50 us -> 0 us
  local copies, waits for them, and re-layouts: 34.2 us -> 3.05 us
  matrix products: 21.9 us -> 0 us
  other arithmetic: 9.13 us -> 0 us
  starting transfers between devices: 6.22 us -> 0 us
    pallas_call x0 -> x1, Pallas kernels: none -> 117 us  [experts_layer(): pl.pallas_call(experts_kernel, out_shape=jax.ShapeDtypeStruct((TOK, WIDTH...]
    all_to_all x1 -> x0, blocking collectives: 61.9 us -> none  [body(): lax.all_to_all(outgoing, ('seq', 'exp'), split_axis=0, concat_axis=0, til...]
    all_to_all x1 -> x0, waiting for transfers between devices: 50 us -> none  [body(): lax.all_to_all(result, ('seq', 'exp'), split_axis=0, concat_axis=0, tiled...]
    reshape x4 -> x0, local copies, waits for them, and re-layouts: 25.1 us -> none  [the longest x1 6.32 us: body(): back = back.reshape(nexp * capacity, width)]
    dot_general x4 -> x0, matrix products: 21.9 us -> none  [the longest x1 11 us: expert_token_rows(): jnp.dot(act, down_proj[0], preferred_element_type=jnp.float32)]
    gather x1 -> x0, local copies, waits for them, and re-layouts: 7.51 us -> none  [body(): gathered = back[slot].reshape(tokens, TOPK, width)]
    all_to_all x1 -> x0, starting transfers between devices: 6.22 us -> none  [body(): lax.all_to_all(result, ('seq', 'exp'), split_axis=0, concat_axis=0, tiled...]
    reduce_sum x5 -> x0, other arithmetic: 5.18 us -> none  [the longest x1 3.43 us: body(): moe = jnp.sum(gates[:, :, None] * gathered.astype(jnp.float32), axis=1)]
  transfers between devices with their start and end apart: 1 -> 0, of which waited for: 1 -> 0; matrix products, arithmetic and copies ran while one was open for 1% -> 0% of each run, Pallas kernels for 0% -> 0%
where the time goes in v2:
time: 183 us; the launch traced here: 181 us
  Pallas kernels  178 us (97%)
  local copies, waits for them, and re-layouts  3.05 us (2%)
    pallas_call x1, Pallas kernels, experts_layer(): pl.pallas_call(experts_kernel, out_shape=jax.ShapeDtypeStruct((TOK, WIDTH...  117 us
    pallas_call x1, Pallas kernels, attention_mixed(): pl.pallas_call(attention_kernel, out_shape=jax.ShapeDtypeStruct((TOK, WID...  60.9 us

profile of v2, /device:TPU:1, one launch (start us, length us, event | category | flops | bytes accessed | tf_op | source)
XLA Modules:
  0.0 181.4 jit_solution(16238362445359602766)
XLA Ops:
  0.7 1.4 copy.15
  2.0 60.9 %attention_exchange.1.mixed_hbm = f32[64,2048]{1,0:T(8,128)} custom-call(s32[1]{0:T(128)S(6)} %copy.17.len_ref, bf16[64,4096]{1,0:T(8,128)(2,1)} %bitcast.16, bf16[64,512]{1,0:T(8,128)(2,1)} %bitcast.21, bf16[64,512]{1,0:T(8,128)(2,1)} %bitcast.22, bf16[512,512]{1,0:T(8,128)(2,1)} %bitcast.17, bf16[512,512]{1,0:T(8,128)(2,1)} %bitcast.18, ...), custom_call_target="tpu_custom_call" | custom-call | tf_op jit(solution)/shard_map/attention_exchange/pallas_call | solution.py:227
  62.9 116.7 %experts_exchange.1 = bf16[64,2048]{1,0:T(8,128)(2,1)} custom-call(f32[64,2048]{1,0:T(8,128)} %attention_exchange.1.mixed_hbm, f32[1,2048]{1,0:T(1,128)} %bitcast.23, bf16[2048,128]{1,0:T(8,128)(2,1)} %router_ref.1, s32[64,8]{1,0:T(8,128)} %bitcast.20, bf16[2048,768]{1,0:T(8,128)(2,1)} %bitcast.12, bf16[2048,768]{1,0:T(8,128)(2,1)} %bitcast.13, ...), custom_call_target="tpu_custom_call" | custom-call | tf_op jit(solution)/shard_map/experts_exchange/pallas_call | solution.py:509
  179.7 1.7 copy.18

commit v3 on v0

v3 whole, which is shorter than its diff:
```python
import jax
import jax.numpy as jnp
from jax import lax
from jax.experimental import pallas as pl
from jax.experimental.pallas import tpu as pltpu
from jax.sharding import PartitionSpec as P

QH = 32
KVH = 4
HD = 128
TOPK = 8
NSEQ = 8
TOK = 64
DOCTOK = 512
CDEV = 512
WIDTH = 2048
LOG2E = 1.4426950408889634
MESH = pl.DeviceIdType.MESH


EXPERTS = 128
FF = 768
PEERS = 16
SLOTS = 48
CAP = 6
ROWS = PEERS * SLOTS
NCHUNK = 4
CHUNK = WIDTH // NCHUNK
NT = (((1,), (1,)), ((), ()))


def layer_kernel(
    len_ref, ids_ref, gain_ref, q_hbm, kn_hbm, vn_hbm, kc_hbm, vc_hbm, w_hbm, res_hbm,
    router_hbm, wg_hbm, wu_hbm, wd_hbm, out_ref,
    qbuf, qext, kbuf, vbuf, acc, mbuf, attn, wbuf, resbuf, router, part,
    sib_out, sib_in, x_out, x_in, sib_in2, x_in2,
    mixed, tokens, table, gtable, pick, give, outbox, relay_out, inbox, relay_back, back,
    rbox, rrelay, rin, wg, wu, wd, hg, hu, act,
    loc_sem, c_send, c_recv, q_send, q_recv, n_send, n_recv, kv_send, kv_recv, fw_send, fw_recv,
    s_send, s_recv, x_send, x_recv, a_send, a_recv, f_send, f_recv, g_send, g_recv,
    d_send, d_recv, r_send, r_recv, s2_send, s2_recv, x2_send, x2_recv,
):
    me = lax.axis_index("seq")
    ex = lax.axis_index("exp")
    x, c = me // 2, lax.rem(me, 2)
    y, z = ex // 4, lax.rem(ex, 4)
    other = 1 - c
    sibling = (2 * x + other, ex)
    f32, bf = jnp.float32, jnp.bfloat16
    everything = []

    def chip(d):
        return lax.rem(x + d, 4)

    def along_x(d):
        return (2 * chip(d) + c, ex)

    def along_y(d):
        return (me, lax.rem(y + d, 4) * 4 + z)

    def along_z(d):
        return (me, y * 4 + lax.rem(z + d, 4))

    def in_row(d):
        return (lax.rem(me + d, NSEQ), ex)

    def block(s):
        return pl.ds(pl.multiple_of(s * TOK, TOK), TOK)

    def cached(s):
        return pl.ds(pl.multiple_of(s * CDEV, CDEV), CDEV)

    def fresh(s):
        return pl.ds(pl.multiple_of(NSEQ * CDEV + s * TOK, TOK), TOK)

    def head(h):
        return pl.ds(pl.multiple_of(h * HD, HD), HD)

    def span(k):
        return pl.ds(k * CHUNK, CHUNK)

    def send(src, dst, sends, recvs, to):
        cp = pltpu.make_async_remote_copy(
            src_ref=src, dst_ref=dst, send_sem=sends, recv_sem=recvs,
            device_id=to, device_id_type=MESH,
        )
        cp.start()
        everything.append(cp)
        return cp

    def fetch(i, src, dst):
        cp = pltpu.make_async_copy(src, dst, loc_sem.at[i])
        cp.start()
        return cp

    barrier = pltpu.get_barrier_semaphore()
    for d in range(1, NSEQ):
        pl.semaphore_signal(barrier, inc=1, device_id=in_row(d), device_id_type=MESH)
    for d in range(1, 4):
        pl.semaphore_signal(barrier, inc=1, device_id=along_y(d), device_id_type=MESH)
        pl.semaphore_signal(barrier, inc=1, device_id=along_z(d), device_id_type=MESH)

    lanes = pl.ds(0, HD)
    own_q = fetch(0, q_hbm.at[:, pl.ds(pl.multiple_of(me * 512, 512), 512)], qbuf.at[block(me), :])
    own_kn = fetch(1, kn_hbm.at[:, head(x)], kbuf.at[fresh(me), lanes])
    own_vn = fetch(2, vn_hbm.at[:, head(x)], vbuf.at[fresh(me), lanes])
    own_k = fetch(3, kc_hbm.at[:, head(x)], kbuf.at[cached(me), lanes])
    own_v = fetch(4, vc_hbm.at[:, head(x)], vbuf.at[cached(me), lanes])

    lane = lax.broadcasted_iota(jnp.int32, (TOK, EXPERTS), 1)
    chosen = jnp.zeros((TOK, EXPERTS), f32)
    for k in range(TOPK):
        chosen = chosen + jnp.where(ids_ref[:, k:k + 1] == lane, f32(1.0), f32(0.0))
    before = (lax.broadcasted_iota(jnp.int32, (TOK, TOK), 1)
              < lax.broadcasted_iota(jnp.int32, (TOK, TOK), 0)).astype(f32)
    rank = jnp.dot(before.astype(bf), chosen.astype(bf), preferred_element_type=f32)
    first = (CAP * me + 1).astype(f32)
    table[block(me), :] = jnp.where(chosen > 0, rank + first, f32(0.0)).astype(bf)

    pl.semaphore_wait(barrier, NSEQ - 1 + 6)
    q_copies, n_copies, c_copies = [], [], []
    for d in (4, 2, 6, 3, 5, 1, 7):
        to = lax.rem(me + d, NSEQ)
        q_copies.append(send(
            q_hbm.at[:, pl.ds(pl.multiple_of(to * 512, 512), 512)], qbuf.at[block(me), :],
            q_send.at[d], q_recv.at[d], in_row(d)))
    for d in (4, 2, 6, 3, 5, 1, 7):
        h = lax.rem(me + d, NSEQ) // 2
        for i, (src, dst) in enumerate(((kn_hbm, kbuf), (vn_hbm, vbuf))):
            n_copies.append(send(
                src.at[:, head(h)], dst.at[fresh(me), lanes],
                n_send.at[d, i], n_recv.at[d, i], in_row(d)))
    fw_copies = {0: [
        send(src.at[:, head(x)], dst.at[cached(me), lanes],
             fw_send.at[0, i], fw_recv.at[0, i], sibling)
        for i, (src, dst) in enumerate(((kc_hbm, kbuf), (vc_hbm, vbuf)))
    ]}
    kv_copies = {}
    for d in (1, 3, 2):
        kv_copies[d] = [
            send(src.at[:, head(chip(d))], dst.at[cached(me), lanes],
                 kv_send.at[d, i], kv_recv.at[d, i], along_x(d))
            for i, (src, dst) in enumerate(((kc_hbm, kbuf), (vc_hbm, vbuf)))
        ]
    for d in range(1, NSEQ):
        view = table.at[block(me), :]
        c_copies.append(send(view, view, c_send.at[d], c_recv.at[d], in_row(d)))
    get_w = fetch(5, w_hbm, wbuf)
    get_res = fetch(6, res_hbm, resbuf)
    get_router = fetch(7, router_hbm, router)
    get_wg = fetch(8, wg_hbm, wg)
    get_wu = fetch(9, wu_hbm, wu)
    get_wd = fetch(10, wd_hbm, wd)

    total = NSEQ * (CDEV + TOK)
    lane = lax.broadcasted_iota(jnp.int32, (total, HD), 1)
    pos = lax.broadcasted_iota(jnp.int32, (total, HD), 0)
    hidden = (pos >= len_ref[0]) & (pos < NSEQ * CDEV) & (lane == 0)
    kbuf[:, HD:] = jnp.where(hidden, f32(-1e30), f32(0.0)).astype(bf)
    vbuf[:, HD:] = jnp.ones((total, HD), bf)
    acc[...] = jnp.zeros_like(acc)
    mbuf[...] = jnp.full(mbuf.shape, -3e38, f32)
    unit = (lax.broadcasted_iota(jnp.int32, (DOCTOK, HD), 1) == 0).astype(f32).astype(bf)
    for h in range(4):
        qext[h, :, HD:] = unit

    for cp in q_copies:
        cp.wait_recv()
    own_q.wait()
    for h in range(4):
        qext[h, :, :HD] = qbuf[:, h * HD:(h + 1) * HD]

    factor = f32(LOG2E / (HD ** 0.5))

    def attend(begin, count, causal):
        keys_at = pl.ds(begin, count)

        def one_head(h, carry):
            for half in range(2):
                rows = pl.ds(half * 256, 256)
                s = lax.dot_general(
                    qext[h, rows, :], kbuf[keys_at, :], NT, preferred_element_type=f32
                )
                if causal:
                    t = lax.broadcasted_iota(jnp.int32, s.shape, 0) + half * 256
                    u = lax.broadcasted_iota(jnp.int32, s.shape, 1)
                    s = jnp.where(u <= t, s, f32(-1e30))
                m_old = mbuf[h, rows, :]
                m_new = jnp.maximum(m_old, jnp.max(s, axis=1, keepdims=True))
                mbuf[h, rows, :] = m_new
                alpha = jnp.exp2((m_old - m_new) * factor)
                p = jnp.exp2((s - m_new[:, :1]) * factor).astype(bf)
                pv = jnp.dot(p, vbuf[keys_at, :], preferred_element_type=f32)
                acc[h, rows, :HD] = acc[h, rows, :HD] * alpha + pv[:, :HD]
                acc[h, rows, HD:] = acc[h, rows, HD:] * alpha + pv[:, HD:]
            return carry

        lax.fori_loop(0, 4, one_head, 0)

    def forward_kv(d):
        for cp in kv_copies[d]:
            cp.wait_recv()
        src = 2 * lax.rem(x + 4 - d, 4) + c
        fw_copies[d] = [
            send(view, view, fw_send.at[d, i], fw_recv.at[d, i], sibling)
            for i, view in enumerate((kbuf.at[cached(src), lanes], vbuf.at[cached(src), lanes]))
        ]

    def attend_chip(d):
        for cp in fw_copies[d]:
            cp.wait_recv()
        attend(pl.multiple_of(lax.rem(x + 4 - d, 4) * 1024, 1024), 1024, False)

    own_k.wait()
    own_v.wait()
    attend_chip(0)
    own_kn.wait()
    own_vn.wait()
    for cp in n_copies:
        cp.wait_recv()
    attend(NSEQ * CDEV, DOCTOK, True)
    forward_kv(1)
    forward_kv(3)

    qi = lax.broadcasted_iota(jnp.int32, (ROWS, EXPERTS), 0)
    ei = (lax.broadcasted_iota(jnp.int32, (ROWS, EXPERTS), 1) - me * PEERS) * SLOTS
    owner = jnp.where((qi >= ei) & (qi < ei + SLOTS), f32(1.0), f32(0.0)).astype(bf)

    def within(shape, axis):
        at = lax.broadcasted_iota(jnp.int32, shape, axis)
        low = at + 1
        for e in range(1, PEERS):
            low = jnp.where(at >= e * SLOTS, at + 1 - e * SLOTS, low)
        return low.astype(f32)

    for cp in c_copies:
        cp.wait_recv()
    by_row = lax.dot_general(owner, table[...], NT, preferred_element_type=f32)
    pick[...] = jnp.where(by_row == within((ROWS, 128), 0)[:, :1], f32(1.0), f32(0.0)).astype(bf)

    attend_chip(1)
    forward_kv(2)
    attend_chip(3)
    attend_chip(2)

    get_w.wait()
    get_res.wait()
    get_router.wait()
    for d in range(4):
        for i, core in enumerate((other, c)):
            at = block(2 * chip(d) + core)
            for h in range(4):
                attn[i, d, :, h * HD:(h + 1) * HD] = (
                    acc[h, at, :HD] / acc[h, at, HD:]
                ).astype(bf)

    s_copies, x_copies = {}, {}

    def sum_cores(k):
        sib_out[:, :, span(k)] = jnp.dot(
            attn[0].reshape(4 * TOK, 512), wbuf[:, span(k)], preferred_element_type=f32
        ).astype(bf).reshape(4, TOK, CHUNK)
        view = sib_out.at[:, :, span(k)]
        s_copies[k] = send(view, sib_in.at[:, :, span(k)], s_send.at[k], s_recv.at[k], sibling)
        part[:, :, span(k)] = jnp.dot(
            attn[1].reshape(4 * TOK, 512), wbuf[:, span(k)], preferred_element_type=f32
        ).reshape(4, TOK, CHUNK)

    def sum_chips(k):
        s_copies[k].wait_recv()
        x_copies[k] = []
        for d in (2, 1, 3):
            x_out[d, :, span(k)] = (
                part[d, :, span(k)] + sib_in[d, :, span(k)].astype(f32)
            ).astype(bf)
            x_copies[k].append(send(
                x_out.at[d, :, span(k)], x_in.at[d, :, span(k)],
                x_send.at[k, d], x_recv.at[k, d], along_x(d)))

    a_copies, f_copies = {}, {}

    def spread(k):
        mine = (resbuf[:, span(k)].astype(f32) + part[0, :, span(k)]
                + sib_in[0, :, span(k)].astype(f32))
        for cp in x_copies[k]:
            cp.wait_recv()
        for d in (1, 2, 3):
            mine = mine + x_in[d, :, span(k)].astype(f32)
        mixed[:, span(k)] = mine
        tokens[block(me), span(k)] = (mine * gain_ref[:, span(k)]).astype(bf)
        view = tokens.at[block(me), span(k)]
        a_copies[k] = {
            d: send(view, view, a_send.at[k, d], a_recv.at[k, d],
                    sibling if d == 0 else along_x(d))
            for d in (2, 1, 3, 0)
        }

    def forward(k):
        f_copies[k] = []
        for d in (1, 3, 2):
            a_copies[k][d].wait_recv()
            view = tokens.at[block(2 * lax.rem(x + 4 - d, 4) + c), span(k)]
            f_copies[k].append(send(view, view, f_send.at[k, d], f_recv.at[k, d], sibling))

    def hop(even, at, source, target, sends, recvs, base):
        copies = []
        for d in (1, 3, 2):
            if even:
                src, dst, to = source.at[lax.rem(y + d, 4), :, :, at], target.at[y, :, :, at], along_y(d)
            else:
                src, dst, to = source.at[:, lax.rem(z + d, 4), :, at], target.at[:, z, :, at], along_z(d)
            copies.append(send(src, dst, sends.at[base + d], recvs.at[base + d], to))
        if even:
            target[y, :, :, at] = source[y, :, :, at]
        else:
            target[:, z, :, at] = source[:, z, :, at]
        return copies

    d_first, d_second, r_first, r_second = {}, {}, {}, {}

    def dispatch(k):
        a_copies[k][0].wait_recv()
        for cp in f_copies[k]:
            cp.wait_recv()
        outbox[:, :, :, span(k)] = jnp.dot(
            pick[...], tokens[:, span(k)], preferred_element_type=f32
        ).astype(bf).reshape(4, 4, SLOTS, CHUNK)
        d_first[k] = hop(k % 2 == 0, span(k), outbox, relay_out, d_send, d_recv, 8 * k)

    def dispatch_on(k):
        for cp in d_first[k]:
            cp.wait_recv()
        d_second[k] = hop(k % 2 == 1, span(k), relay_out, inbox, d_send, d_recv, 8 * k + 4)

    stages = (sum_cores, sum_chips, spread, forward, dispatch)
    for t in range(NCHUNK + len(stages) - 1):
        for i, stage in enumerate(stages):
            if 0 <= t - i < NCHUNK:
                stage(t - i)
        if t == NCHUNK + 1:
            mx = mixed[...]
            factor_of = f32(1.0) / jnp.sqrt(jnp.mean(mx * mx, axis=1, keepdims=True) + 1e-06)
            normed = (mx * factor_of * gain_ref[...]).astype(bf)
            logits = jnp.dot(normed, router[...], preferred_element_type=f32)
            expo = jnp.where(chosen > 0, jnp.exp(logits), f32(0.0))
            gtable[block(me), :EXPERTS] = expo / jnp.sum(expo, axis=1, keepdims=True)
            gtable[block(me), EXPERTS:] = jnp.broadcast_to(factor_of, (TOK, EXPERTS))
            view = gtable.at[block(me), :]
            g_copies = [
                send(view, view, g_send.at[d], g_recv.at[d], in_row(d)) for d in range(1, NSEQ)
            ]
        if t == NCHUNK + 2:
            dispatch_on(0)

    for cp in g_copies:
        cp.wait_recv()
    fac = gtable[:, EXPERTS:]
    high = fac.astype(bf)
    rest = fac - high.astype(f32)
    mid = rest.astype(bf)
    low = (rest - mid.astype(f32)).astype(bf)
    by_slot = (jnp.dot(pick[...], high, preferred_element_type=f32)
               + jnp.dot(pick[...], mid, preferred_element_type=f32)
               + jnp.dot(pick[...], low, preferred_element_type=f32))
    slot_lane = lax.broadcasted_iota(jnp.int32, (PEERS, SLOTS, 128), 2)
    slot_row = lax.broadcasted_iota(jnp.int32, (PEERS, SLOTS, 128), 1)
    lined = jnp.sum(
        jnp.where(slot_lane == slot_row, by_slot.reshape(PEERS, SLOTS, 128), f32(0.0)), axis=1
    )
    rbox[...] = jnp.broadcast_to(lined[:, None, :], (PEERS, 8, 128)).reshape(4, 4, 8, 128)
    every = pl.ds(0, 128)
    rf = hop(True, every, rbox, rrelay, d_send, d_recv, 8 * NCHUNK)

    dispatch_on(1)
    dispatch_on(2)
    dispatch_on(3)
    for cp in rf:
        cp.wait_recv()
    rs = hop(False, every, rrelay, rin, d_send, d_recv, 8 * NCHUNK + 4)

    by_token = lax.dot_general(table[...], owner, NT, preferred_element_type=f32)
    share = lax.dot_general(gtable[:, :EXPERTS].astype(bf), owner, NT, preferred_element_type=f32)
    give[...] = jnp.where(by_token == within((8, ROWS), 1)[:1, :], share, f32(0.0)).astype(bf)

    get_wg.wait()
    get_wu.wait()
    for k in range(NCHUNK):
        for cp in d_second[k]:
            cp.wait_recv()
        rows = inbox[:, :, :, span(k)].reshape(ROWS, CHUNK)
        g = jnp.dot(rows, wg[span(k), :], preferred_element_type=f32)
        u = jnp.dot(rows, wu[span(k), :], preferred_element_type=f32)
        if k == 0:
            hg[...] = g
            hu[...] = u
        else:
            hg[...] += g
            hu[...] += u
    for cp in rs:
        cp.wait_recv()
    got = rin[...].reshape(PEERS, 8, 128)[:, :1, :]
    scale = jnp.sum(jnp.where(slot_lane == slot_row, got, f32(0.0)), axis=2, keepdims=True)
    scale = scale.reshape(ROWS, 1)
    g = hg[...] * scale
    act[...] = (g / (f32(1.0) + jnp.exp(-g)) * (hu[...] * scale)).astype(bf)
    get_wd.wait()
    reused = [cp for k in range(NCHUNK) for cp in d_first[k] + x_copies[k] + [s_copies[k]]]
    for cp in reused:
        cp.wait_send()
    for k in range(NCHUNK):
        outbox[:, :, :, span(k)] = jnp.dot(
            act[...], wd[:, span(k)], preferred_element_type=f32
        ).astype(bf).reshape(4, 4, SLOTS, CHUNK)
        r_first[k] = hop(k % 2 == 0, span(k), outbox, relay_back, r_send, r_recv, 8 * k)

    for k in range(NCHUNK):
        for cp in r_first[k]:
            cp.wait_recv()
        r_second[k] = hop(k % 2 == 1, span(k), relay_back, back, r_send, r_recv, 8 * k + 4)

    s2_copies, x2_copies = {}, {}

    def combine(k):
        for cp in r_second[k]:
            cp.wait_recv()
        returned = back[:, :, :, span(k)].reshape(ROWS, CHUNK)
        for d in (2, 1, 3, 0):
            sib_out[d, :, span(k)] = jnp.dot(
                give[block(2 * chip(d) + other), :], returned, preferred_element_type=f32
            ).astype(bf)
        view = sib_out.at[:, :, span(k)]
        s2_copies[k] = send(view, sib_in2.at[:, :, span(k)], s2_send.at[k], s2_recv.at[k], sibling)
        for d in (2, 1, 3, 0):
            part[d, :, span(k)] = jnp.dot(
                give[block(2 * chip(d) + c), :], returned, preferred_element_type=f32
            )

    def combine_chips(k):
        s2_copies[k].wait_recv()
        x2_copies[k] = []
        for d in (2, 1, 3):
            x_out[d, :, span(k)] = (
                part[d, :, span(k)] + sib_in2[d, :, span(k)].astype(f32)
            ).astype(bf)
            x2_copies[k].append(send(
                x_out.at[d, :, span(k)], x_in2.at[d, :, span(k)],
                x2_send.at[k, d], x2_recv.at[k, d], along_x(d)))

    for k in range(NCHUNK):
        combine(k)
        if k:
            combine_chips(k - 1)
    combine_chips(NCHUNK - 1)
    for k in range(NCHUNK):
        out = mixed[:, span(k)] + part[0, :, span(k)] + sib_in2[0, :, span(k)].astype(f32)
        for cp in x2_copies[k]:
            cp.wait_recv()
        for d in (1, 2, 3):
            out = out + x_in2[d, :, span(k)].astype(f32)
        out_ref[:, span(k)] = out.astype(bf)

    for cp in everything:
        if not any(cp is done for done in reused):
            cp.wait_send()


def layer(
    queries, new_keys, new_values, cache_keys, cache_values, cache_len, residual_in,
    out_weight, norm_gain, router_weight, expert_ids, gate_proj, up_proj, down_proj,
):
    hbm = pl.BlockSpec(memory_space=pl.ANY)
    vmem = pl.BlockSpec(memory_space=pltpu.VMEM)
    bf, f32 = jnp.bfloat16, jnp.float32
    dma = pltpu.SemaphoreType.DMA
    total = NSEQ * (CDEV + TOK)
    plane = pltpu.VMEM((4, 4, SLOTS, WIDTH), bf)
    small = pltpu.VMEM((4, 4, 8, 128), f32)
    row = pltpu.VMEM((4, TOK, WIDTH), bf)
    out = pl.pallas_call(
        layer_kernel,
        out_shape=jax.ShapeDtypeStruct((TOK, WIDTH), bf),
        in_specs=[pl.BlockSpec(memory_space=pltpu.SMEM), vmem, vmem] + [hbm] * 11,
        out_specs=vmem,
        scratch_shapes=[
            pltpu.VMEM((DOCTOK, 512), bf),
            pltpu.VMEM((4, DOCTOK, 256), bf),
            pltpu.VMEM((total, 256), bf),
            pltpu.VMEM((total, 256), bf),
            pltpu.VMEM((4, DOCTOK, 256), f32),
            pltpu.VMEM((4, DOCTOK, HD), f32),
            pltpu.VMEM((2, 4, TOK, 512), bf),
            pltpu.VMEM((512, WIDTH), bf),
            pltpu.VMEM((TOK, WIDTH), bf),
            pltpu.VMEM((WIDTH, EXPERTS), bf),
            pltpu.VMEM((4, TOK, WIDTH), f32),
            row, row, row, row, row, row,
            pltpu.VMEM((TOK, WIDTH), f32),
            pltpu.VMEM((DOCTOK, WIDTH), bf),
            pltpu.VMEM((DOCTOK, EXPERTS), bf),
            pltpu.VMEM((DOCTOK, 2 * EXPERTS), f32),
            pltpu.VMEM((ROWS, DOCTOK), bf),
            pltpu.VMEM((DOCTOK, ROWS), bf),
            plane, plane, plane, plane, plane,
            small, small, small,
            pltpu.VMEM((WIDTH, FF), bf),
            pltpu.VMEM((WIDTH, FF), bf),
            pltpu.VMEM((FF, WIDTH), bf),
            pltpu.VMEM((ROWS, FF), f32),
            pltpu.VMEM((ROWS, FF), f32),
            pltpu.VMEM((ROWS, FF), bf),
            dma((11,)), dma((8,)), dma((8,)), dma((8,)), dma((8,)), dma((8, 2)), dma((8, 2)),
            dma((4, 2)), dma((4, 2)), dma((4, 2)), dma((4, 2)),
            dma((NCHUNK,)), dma((NCHUNK,)), dma((NCHUNK, 4)), dma((NCHUNK, 4)),
            dma((NCHUNK, 4)), dma((NCHUNK, 4)), dma((NCHUNK, 4)), dma((NCHUNK, 4)),
            dma((8,)), dma((8,)),
            dma((8 * NCHUNK + 8,)), dma((8 * NCHUNK + 8,)), dma((8 * NCHUNK,)), dma((8 * NCHUNK,)),
            dma((NCHUNK,)), dma((NCHUNK,)), dma((NCHUNK, 4)), dma((NCHUNK, 4)),
        ],
        compiler_params=pltpu.CompilerParams(
            collective_id=0, has_side_effects=True, vmem_limit_bytes=67043328
        ),
        name="whole_layer",
    )(cache_len, expert_ids[0], norm_gain.reshape(1, WIDTH), queries[0], new_keys[0],
      new_values[0], cache_keys[0], cache_values[0], out_weight, residual_in[0],
      router_weight, gate_proj[0], up_proj[0], down_proj[0])
    return out.reshape(1, TOK, WIDTH)


def solution(mesh):
    in_specs = (
        P("exp", "seq", None),
        P("exp", "seq", None),
        P("exp", "seq", None),
        P("exp", "seq", None),
        P("exp", "seq", None),
        P("exp"),
        P("exp", "seq", None),
        P("seq", None),
        P(),
        P(),
        P("exp", "seq", None),
        P(("seq", "exp"), None, None),
        P(("seq", "exp"), None, None),
        P(("seq", "exp"), None, None),
    )
    out_specs = P("exp", "seq", None)
    return jax.shard_map(layer, mesh=mesh, in_specs=in_specs, out_specs=out_specs, check_vma=False)
```

time: 374 us -> 167 us (0.45)
  Pallas kernels: 0 us -> 163 us
  waiting for transfers between devices: 112 us -> 0 us
  matrix products: 63.6 us -> 0 us
  blocking collectives: 62.5 us -> 0 us
  local copies, waits for them, and re-layouts: 55.6 us -> 3.05 us
  other arithmetic: 32 us -> 0 us
  starting transfers between devices: 31.2 us -> 0 us
  between operations: 14.2 us -> 0.66 us
    pallas_call x0 -> x1, Pallas kernels: none -> 163 us  [layer(): pl.pallas_call(layer_kernel, out_shape=jax.ShapeDtypeStruct((TOK, WIDTH),...]
    all_to_all x6 -> x0, waiting for transfers between devices: 80.2 us -> none  [the longest x1 49.9 us: body(): lax.all_to_all(result, ('seq', 'exp'), split_axis=0, concat_axis=0, tiled...]
    dot_general x7 -> x0, matrix products: 63.6 us -> none  [the longest x1 18.9 us: attend(): jnp.einsum('pgbk,kpd->bpgd', weight_matrices, value_entries, preferred_el...]
    all_to_all x1 -> x0, blocking collectives: 62.5 us -> none  [body(): lax.all_to_all(outgoing, ('seq', 'exp'), split_axis=0, concat_axis=0, til...]
    reduce_scatter x1 -> x0, waiting for transfers between devices: 32.1 us -> none  [body(): lax.psum_scatter(jnp.dot(attn, out_weight, preferred_element_type=jnp.flo...]
    all_to_all x6 -> x0, starting transfers between devices: 31.2 us -> none  [the longest x1 6.22 us: body(): lax.all_to_all(result, ('seq', 'exp'), split_axis=0, concat_axis=0, tiled...]
    reshape x4 -> x0, local copies, waits for them, and re-layouts: 25.2 us -> none  [the longest x1 6.34 us: expert_token_rows(): rows = piece.reshape(-1, width)]
    reduce_sum x6 -> x0, other arithmetic: 21.3 us -> none  [the longest x1 16.1 us: attend(): jnp.sum(expo, axis=-1, keepdims=True)]
  transfers between devices with their start and end apart: 7 -> 0, of which waited for: 7 -> 0; matrix products, arithmetic and copies ran while one was open for 6% -> 0% of each run, Pallas kernels for 0% -> 0%
where the time goes in v3:
time: 167 us
  Pallas kernels  163 us (98%)
  local copies, waits for them, and re-layouts  3.05 us (2%)
    pallas_call x1, Pallas kernels, layer(): pl.pallas_call(layer_kernel, out_shape=jax.ShapeDtypeStruct((TOK, WIDTH),...  163 us

profile of v3, /device:TPU:1, one launch (start us, length us, event | category | flops | bytes accessed | tf_op | source)
XLA Modules:
  0.0 166.6 jit_solution(411038428519273695)
XLA Ops:
  0.7 1.4 copy.15
  2.0 162.9 %whole_layer.1 = bf16[64,2048]{1,0:T(8,128)(2,1)} custom-call(s32[1]{0:T(128)S(6)} %copy.17.len_ref, s32[64,8]{1,0:T(8,128)} %bitcast.20, f32[1,2048]{1,0:T(1,128)} %bitcast.23, bf16[64,4096]{1,0:T(8,128)(2,1)} %bitcast.16, bf16[64,512]{1,0:T(8,128)(2,1)} %bitcast.21, bf16[64,512]{1,0:T(8,128)(2,1)} %bitcast.22, bf16[512,512]{1,0:T(8,128)(2,1)} %bitcast.17, ...), custom_call_target="tpu_custom_call" | custom-call | tf_op jit(solution)/shard_map/whole_layer/pallas_call | solution.py:479
  164.9 1.7 %copy.18 = bf16[1,64,2048]{2,1,0:T(8,128)(2,1)} copy(bf16[1,64,2048]{2,1,0:T(8,128)(2,1)} %bitcast.15) | data formatting | bytes 524288

commit v4 on v3

--- a/solution.py
+++ b/solution.py
@@ -26,6 +26,7 @@
 ROWS = PEERS * SLOTS
 NCHUNK = 4
 CHUNK = WIDTH // NCHUNK
+AHEAD = 6
 NT = (((1,), (1,)), ((), ()))
 
 
@@ -175,16 +176,20 @@
     def attend(begin, count, causal):
         keys_at = pl.ds(begin, count)
 
-        def one_head(h, carry):
-            for half in range(2):
-                rows = pl.ds(half * 256, 256)
+        def heads_of(i, carry):
+            tiles = [(i * 2 + j, r * 256) for j in range(2) for r in range(2)]
+            scores = []
+            for h, r in tiles:
                 s = lax.dot_general(
-                    qext[h, rows, :], kbuf[keys_at, :], NT, preferred_element_type=f32
+                    qext[h, pl.ds(r, 256), :], kbuf[keys_at, :], NT, preferred_element_type=f32
                 )
                 if causal:
-                    t = lax.broadcasted_iota(jnp.int32, s.shape, 0) + half * 256
+                    t = lax.broadcasted_iota(jnp.int32, s.shape, 0) + r
                     u = lax.broadcasted_iota(jnp.int32, s.shape, 1)
                     s = jnp.where(u <= t, s, f32(-1e30))
+                scores.append(s)
+            for (h, r), s in zip(tiles, scores):
+                rows = pl.ds(r, 256)
                 m_old = mbuf[h, rows, :]
                 m_new = jnp.maximum(m_old, jnp.max(s, axis=1, keepdims=True))
                 mbuf[h, rows, :] = m_new
@@ -195,7 +200,7 @@
                 acc[h, rows, HD:] = acc[h, rows, HD:] * alpha + pv[:, HD:]
             return carry
 
-        lax.fori_loop(0, 4, one_head, 0)
+        lax.fori_loop(0, 2, heads_of, 0)
 
     def forward_kv(d):
         for cp in kv_copies[d]:
@@ -316,6 +321,13 @@
             target[:, z, :, at] = source[:, z, :, at]
         return copies
 
+    def both(k, turn, source, target, sends, recvs, base):
+        copies = []
+        for i in range(2):
+            at = pl.ds(k * CHUNK + i * (CHUNK // 2), CHUNK // 2)
+            copies += hop((i + turn) % 2 == 0, at, source, target, sends, recvs, base + 4 * i)
+        return copies
+
     d_first, d_second, r_first, r_second = {}, {}, {}, {}
 
     def dispatch(k):
@@ -325,12 +337,12 @@
         outbox[:, :, :, span(k)] = jnp.dot(
             pick[...], tokens[:, span(k)], preferred_element_type=f32
         ).astype(bf).reshape(4, 4, SLOTS, CHUNK)
-        d_first[k] = hop(k % 2 == 0, span(k), outbox, relay_out, d_send, d_recv, 8 * k)
+        d_first[k] = both(k, 0, outbox, relay_out, d_send, d_recv, 16 * k)
 
     def dispatch_on(k):
         for cp in d_first[k]:
             cp.wait_recv()
-        d_second[k] = hop(k % 2 == 1, span(k), relay_out, inbox, d_send, d_recv, 8 * k + 4)
+        d_second[k] = both(k, 1, relay_out, inbox, d_send, d_recv, 16 * k + 8)
 
     stages = (sum_cores, sum_chips, spread, forward, dispatch)
     for t in range(NCHUNK + len(stages) - 1):
@@ -349,8 +361,8 @@
             g_copies = [
                 send(view, view, g_send.at[d], g_recv.at[d], in_row(d)) for d in range(1, NSEQ)
             ]
-        if t == NCHUNK + 2:
-            dispatch_on(0)
+        if t >= AHEAD:
+            dispatch_on(t - AHEAD)
 
     for cp in g_copies:
         cp.wait_recv()
@@ -369,14 +381,13 @@
     )
     rbox[...] = jnp.broadcast_to(lined[:, None, :], (PEERS, 8, 128)).reshape(4, 4, 8, 128)
     every = pl.ds(0, 128)
-    rf = hop(True, every, rbox, rrelay, d_send, d_recv, 8 * NCHUNK)
-
-    dispatch_on(1)
-    dispatch_on(2)
-    dispatch_on(3)
+    rf = hop(True, every, rbox, rrelay, d_send, d_recv, 16 * NCHUNK)
+
+    for k in range(NCHUNK + 4 - AHEAD, NCHUNK):
+        dispatch_on(k)
     for cp in rf:
         cp.wait_recv()
-    rs = hop(False, every, rrelay, rin, d_send, d_recv, 8 * NCHUNK + 4)
+    rs = hop(False, every, rrelay, rin, d_send, d_recv, 16 * NCHUNK + 4)
 
     by_token = lax.dot_general(table[...], owner, NT, preferred_element_type=f32)
     share = lax.dot_general(gtable[:, :EXPERTS].astype(bf), owner, NT, preferred_element_type=f32)
@@ -411,12 +422,12 @@
         outbox[:, :, :, span(k)] = jnp.dot(
             act[...], wd[:, span(k)], preferred_element_type=f32
         ).astype(bf).reshape(4, 4, SLOTS, CHUNK)
-        r_first[k] = hop(k % 2 == 0, span(k), outbox, relay_back, r_send, r_recv, 8 * k)
+        r_first[k] = both(k, 0, outbox, relay_back, r_send, r_recv, 16 * k)
 
     for k in range(NCHUNK):
         for cp in r_first[k]:
             cp.wait_recv()
-        r_second[k] = hop(k % 2 == 1, span(k), relay_back, back, r_send, r_recv, 8 * k + 4)
+        r_second[k] = both(k, 1, relay_back, back, r_send, r_recv, 16 * k + 8)
 
     s2_copies, x2_copies = {}, {}
 
@@ -513,7 +524,7 @@
             dma((NCHUNK,)), dma((NCHUNK,)), dma((NCHUNK, 4)), dma((NCHUNK, 4)),
             dma((NCHUNK, 4)), dma((NCHUNK, 4)), dma((NCHUNK, 4)), dma((NCHUNK, 4)),
             dma((8,)), dma((8,)),
-            dma((8 * NCHUNK + 8,)), dma((8 * NCHUNK + 8,)), dma((8 * NCHUNK,)), dma((8 * NCHUNK,)),
+            dma((16 * NCHUNK + 8,)), dma((16 * NCHUNK + 8,)), dma((16 * NCHUNK,)), dma((16 * NCHUNK,)),
             dma((NCHUNK,)), dma((NCHUNK,)), dma((NCHUNK, 4)), dma((NCHUNK, 4)),
         ],
         compiler_params=pltpu.CompilerParams(

time: 167 us -> 156 us (0.934)
  Pallas kernels: 163 us -> 152 us
    pallas_call x1, Pallas kernels: 163 us -> 152 us  [layer(): pl.pallas_call(layer_kernel, out_shape=jax.ShapeDtypeStruct((TOK, WIDTH),...]
where the time goes in v4:
time: 156 us; the launch traced here: 155 us
  Pallas kernels  152 us (97%)
  local copies, waits for them, and re-layouts  3.05 us (2%)
    pallas_call x1, Pallas kernels, layer(): pl.pallas_call(layer_kernel, out_shape=jax.ShapeDtypeStruct((TOK, WIDTH),...  152 us

profile of v4, /device:TPU:1, one launch (start us, length us, event | category | flops | bytes accessed | tf_op | source)
XLA Modules:
  0.0 155.3 jit_solution(9159710104830488878)
XLA Ops:
  0.7 1.4 copy.15
  2.0 151.6 %whole_layer.1 = bf16[64,2048]{1,0:T(8,128)(2,1)} custom-call(s32[1]{0:T(128)S(6)} %copy.17.len_ref, s32[64,8]{1,0:T(8,128)} %bitcast.20, f32[1,2048]{1,0:T(1,128)} %bitcast.23, bf16[64,4096]{1,0:T(8,128)(2,1)} %bitcast.16, bf16[64,512]{1,0:T(8,128)(2,1)} %bitcast.21, bf16[64,512]{1,0:T(8,128)(2,1)} %bitcast.22, bf16[512,512]{1,0:T(8,128)(2,1)} %bitcast.17, ...), custom_call_target="tpu_custom_call" | custom-call | tf_op jit(solution)/shard_map/whole_layer/pallas_call | solution.py:490
  153.7 1.7 %copy.18 = bf16[1,64,2048]{2,1,0:T(8,128)(2,1)} copy(bf16[1,64,2048]{2,1,0:T(8,128)(2,1)} %bitcast.15) | data formatting | bytes 524288

commit v5 on v4

--- a/solution.py
+++ b/solution.py
@@ -108,10 +108,15 @@
     own_k = fetch(3, kc_hbm.at[:, head(x)], kbuf.at[cached(me), lanes])
     own_v = fetch(4, vc_hbm.at[:, head(x)], vbuf.at[cached(me), lanes])
 
-    lane = lax.broadcasted_iota(jnp.int32, (TOK, EXPERTS), 1)
-    chosen = jnp.zeros((TOK, EXPERTS), f32)
+    by_expert = jnp.zeros((EXPERTS, TOK), f32)
+    expert = lax.broadcasted_iota(jnp.int32, (EXPERTS, TOK), 0)
     for k in range(TOPK):
-        chosen = chosen + jnp.where(ids_ref[:, k:k + 1] == lane, f32(1.0), f32(0.0))
+        by_expert = by_expert + jnp.where(ids_ref[k:k + 1, :] == expert, f32(1.0), f32(0.0))
+    same = (lax.broadcasted_iota(jnp.int32, (TOK, TOK), 1)
+            == lax.broadcasted_iota(jnp.int32, (TOK, TOK), 0)).astype(f32)
+    chosen = lax.dot_general(
+        same.astype(bf), by_expert.astype(bf), NT, preferred_element_type=f32
+    )
     before = (lax.broadcasted_iota(jnp.int32, (TOK, TOK), 1)
               < lax.broadcasted_iota(jnp.int32, (TOK, TOK), 0)).astype(f32)
     rank = jnp.dot(before.astype(bf), chosen.astype(bf), preferred_element_type=f32)
@@ -531,7 +536,7 @@
             collective_id=0, has_side_effects=True, vmem_limit_bytes=67043328
         ),
         name="whole_layer",
-    )(cache_len, expert_ids[0], norm_gain.reshape(1, WIDTH), queries[0], new_keys[0],
+    )(cache_len, expert_ids[0].T, norm_gain.reshape(1, WIDTH), queries[0], new_keys[0],
       new_values[0], cache_keys[0], cache_values[0], out_weight, residual_in[0],
       router_weight, gate_proj[0], up_proj[0], down_proj[0])
     return out.reshape(1, TOK, WIDTH)

time: 156 us -> 154 us (0.987)
  no operation moved by 1% of the time
where the time goes in v5:
time: 154 us
  Pallas kernels  152 us (99%)
  local copies, waits for them, and re-layouts  1.67 us (1%)
    pallas_call x1, Pallas kernels, layer(): pl.pallas_call(layer_kernel, out_shape=jax.ShapeDtypeStruct((TOK, WIDTH),...  152 us

profile of v5, /device:TPU:1, one launch (start us, length us, event | category | flops | bytes accessed | tf_op | source)
XLA Modules:
  0.0 154.0 jit_solution(4742554052544070603)
XLA Ops:
  0.7 151.7 %whole_layer.1 = bf16[64,2048]{1,0:T(8,128)(2,1)} custom-call(s32[1]{0:T(128)S(6)} %copy.16.len_ref, s32[8,64]{1,0:T(8,128)} %bitcast.25, f32[1,2048]{1,0:T(1,128)} %bitcast.24, bf16[64,4096]{1,0:T(8,128)(2,1)} %bitcast.18, bf16[64,512]{1,0:T(8,128)(2,1)} %bitcast.22, bf16[64,512]{1,0:T(8,128)(2,1)} %bitcast.23, bf16[512,512]{1,0:T(8,128)(2,1)} %bitcast.19, ...), custom_call_target="tpu_custom_call" | custom-call | tf_op jit(solution)/shard_map/whole_layer/pallas_call | solution.py:495
  152.3 1.7 %copy.17 = bf16[1,64,2048]{2,1,0:T(8,128)(2,1)} copy(bf16[1,64,2048]{2,1,0:T(8,128)(2,1)} %bitcast.17) | data formatting | bytes 524288
